TPU v7x, 32 devices: a whole 2x2x4 slice. The times are simulated.
32 devices in a mesh: groups: 2 (over y), patch: 4 (over z), fsdp: 2 (over x), sub: 2 (over core).
Axes of the slice: x: 2, y: 2, z: 4, core: 2. Of those that a mesh axis runs over, the one named last changes fastest.
Arguments:
- noisy_field: float32 [128, 512], P(('groups', 'patch'), 'sub'), parts along dimension 0, may hold values from -6 to 6
- noise_draw: float32 [128, 512], P(('groups', 'patch'), 'sub'), parts along dimension 0, may hold values from -6 to 6
- cond_features: bfloat16 [128, 512, 128], P(('groups', 'patch'), 'sub'), parts along dimension 0, may hold values from -6 to 6
- sigma_now: float32 [1], replicated, may hold values from 0.5 to 2
- sigma_next: float32 [1], replicated, may hold values from 0.1 to 0.4
- field_proj: float32 [128], replicated, may hold values from -6 to 6
- fine_kernels: bfloat16 [2, 9, 128, 128], replicated, may hold values from -0.1875 to 0.1875
- coarse_kernel: bfloat16 [9, 256, 256], replicated, may hold values from -0.125 to 0.125
- down_proj: bfloat16 [128, 256], replicated, may hold values from -0.5 to 0.5
- up_proj: bfloat16 [256, 128], replicated, may hold values from -0.375 to 0.375
- out_proj: bfloat16 [128], replicated, may hold values from -0.5 to 0.5
Outputs:
- next_field: float32 [128, 512], P(('groups', 'patch'), 'sub'), parts along dimension 0
There are 2 independent parts, one for each index of `groups`. A program takes and returns all parts, laid end to end along the dimension named above; an argument that names none is the same for every part. Nothing has to cross between parts.
All inputs are finite; a program needn't handle non-finite values.
Results may differ from a plain program's by a relative error of at most 0.008.
Values may be sent and summed in bfloat16 or wider, within the bound.
No kernel may reach another device: no remote copies, remote signals or barrier semaphores. Data moves between devices by JAX's collectives and lax.ppermute only.
A program may use at most 64 MiB of HBM per device.

v0:
```python
import jax
import jax.numpy as jnp
from jax import lax
from jax.sharding import PartitionSpec as P


def padded_2(cells, sides, width):
    for axis, dim in sides:
        count = lax.axis_size(axis)
        ends = count - 1
        head = lax.slice_in_dim(cells, 0, width, axis=dim)
        tail = lax.slice_in_dim(cells, cells.shape[dim] - width, cells.shape[dim], axis=dim)
        cells = jnp.concatenate(
            [
                lax.ppermute(tail, axis, [(i, (i + 1) % count) for i in range(ends)]),
                cells,
                lax.ppermute(head, axis, [((i + 1) % count, i) for i in range(ends)]),
            ],
            axis=dim,
        )
    return cells


def tap_sum(padded, kernel, height, breadth):
    summed = jnp.zeros((height, breadth, kernel.shape[2]), jnp.float32)
    for kernel_tap in range(9):
        row_off = kernel_tap // 3
        col_off = kernel_tap % 3
        window = padded[row_off : row_off + height, col_off : col_off + breadth, :]
        summed = summed + jnp.einsum(
            "rci,io->rco", window, kernel[kernel_tap], preferred_element_type=jnp.float32
        )
    return summed


def per_device(
    noisy_field,
    noise_draw,
    cond_features,
    sigma_now,
    sigma_next,
    field_proj,
    fine_kernels,
    coarse_kernel,
    down_proj,
    up_proj,
    out_proj,
):
    height = noisy_field.shape[0]
    breadth = noisy_field.shape[1]
    fine_width = fine_kernels.shape[3]
    level_now = sigma_now[0]
    level_next = sigma_next[0]
    scale_in = 1.0 / jnp.sqrt(level_now * level_now + 1.0)
    scale_skip = 1.0 / (level_now * level_now + 1.0)
    scale_out = level_now * scale_in
    hidden0 = (
        cond_features.astype(jnp.float32) + (scale_in * noisy_field)[:, :, None] * field_proj
    ).astype(jnp.bfloat16)

    def fine_conv(values, layer_index):
        padded = padded_2(values, (("patch", 0), ("sub", 1)), 1)
        return tap_sum(padded, fine_kernels[layer_index], height, breadth)

    hidden1 = (hidden0.astype(jnp.float32) + jax.nn.silu(fine_conv(hidden0, 0))).astype(
        jnp.bfloat16
    )
    pooled = (
        hidden1.astype(jnp.float32)
        .reshape(height // 2, 2, breadth // 2, 2, fine_width)
        .mean(axis=(1, 3))
        .astype(jnp.bfloat16)
    )
    coarse_in = jnp.einsum(
        "rci,io->rco", pooled, down_proj, preferred_element_type=jnp.float32
    ).astype(jnp.bfloat16)
    padded = padded_2(coarse_in, (("patch", 0), ("sub", 1)), 1)
    coarse_out = (
        coarse_in.astype(jnp.float32)
        + jax.nn.silu(tap_sum(padded, coarse_kernel, height // 2, breadth // 2))
    ).astype(jnp.bfloat16)
    lifted = jnp.einsum("rci,io->rco", coarse_out, up_proj, preferred_element_type=jnp.float32)
    lifted = jnp.repeat(jnp.repeat(lifted, 2, axis=0), 2, axis=1)
    hidden2 = (hidden1.astype(jnp.float32) + lifted).astype(jnp.bfloat16)
    hidden3 = (hidden2.astype(jnp.float32) + jax.nn.silu(fine_conv(hidden2, 1))).astype(
        jnp.bfloat16
    )
    network = jnp.sum(hidden3.astype(jnp.float32) * out_proj.astype(jnp.float32), axis=2)
    denoised = scale_skip * noisy_field + scale_out * network
    ratio = level_next / level_now
    spread = jnp.sqrt(level_now * level_now - level_next * level_next)
    return denoised + ratio * (noisy_field - denoised) + spread * noise_draw


def solution(mesh):
    return jax.shard_map(
        per_device,
        mesh=mesh,
        in_specs=(
            P(("groups", "patch"), "sub"),
            P(("groups", "patch"), "sub"),
            P(("groups", "patch"), "sub", None),
            P(),
            P(),
            P(),
            P(),
            P(),
            P(),
            P(),
            P(),
        ),
        out_specs=P(("groups", "patch"), "sub"),
        check_vma=False,
    )
```

profile of v0, /device:TPU:0, one launch (start us, length us, event | category | flops | bytes accessed | tf_op | source)
XLA Modules:
  0.0 76.9 jit_solution(6104613895024720994)
XLA Ops:
  1.5 1.8 %add_convert_fusion.3 = bf16[16,256,128]{2,1,0:T(8,128)(2,1)S(1)} fusion(bf16[16,256,128]{2,1,0:T(8,128)(2,1)} %param.13, f32[128]{0:T(128)} %param.16, f32[16,256]{1,0:T(8,128)S(1)} %broadcast_multiply_fusion), kind=kLoop, calls=%fused_computation.4 | loop fusion | flops 2097152 | bytes 2114048 | tf_op jit(solution)/shard_map/convert_element_type | solution.py:59
  3.2 5.0 %collective-permute-start = (bf16[1,256,128]{2,1,0:T(8,128)(2,1)S(1)}, bf16[1,256,128]{2,1,0:T(8,128)(2,1)S(1)}, u32[]{:S(2)}, u32[]{:S(2)}) collective-permute-start(bf16[1,256,128]{2,1,0:T(8,128)(2,1)S(1)} %get-tuple-element.15), channel_id=1, source_target_pairs={{0,4},{4,8},{8,12},{1,5},{5,9},{9,13},{2,6},{6,10},{10,14},{3,7},{... | collective-permute-start | bytes 196616 | tf_op jit(solution)/shard_map/ppermute | solution.py:15
  8.2 1.3 %collective-permute-start.1 = (bf16[1,256,128]{2,1,0:T(8,128)(2,1)S(1)}, bf16[1,256,128]{2,1,0:T(8,128)(2,1)S(1)}, u32[]{:S(2)}, u32[]{:S(2)}) collective-permute-start(bf16[1,256,128]{2,1,0:T(8,128)(2,1)S(1)} %get-tuple-element.16), channel_id=1, source_target_pairs={{4,0},{8,4},{12,8},{5,1},{9,5},{13,9},{6,2},{10,6},{14,10},{7,3},{... | collective-permute-start | bytes 196616 | tf_op jit(solution)/shard_map/ppermute | solution.py:17
  9.5 2.5 %fusion.115 = f32[16,256,128]{2,1,0:T(8,128)} fusion(bf16[16,256,128]{2,1,0:T(8,128)(2,1)S(1)} %add_convert_fusion.3, bf16[2,9,128,128]{3,2,1,0:T(8,128)(2,1)} %param.17), kind=kOutput, calls=%fused_computation.120 | convolution fusion | flops 134217728 | bytes 3178496 | tf_op jit(solution)/shard_map/rci,io->rco/dot_general | solution.py:30
  12.8 1.5 %collective-permute-done.1 = bf16[1,256,128]{2,1,0:T(8,128)(2,1)S(1)} collective-permute-done((bf16[1,256,128]{2,1,0:T(8,128)(2,1)S(1)}, bf16[1,256,128]{2,1,0:T(8,128)(2,1)S(1)}, u32[]{:S(2)}, u32[]{:S(2)}) %collective-permute-start.1) | collective-permute-done | bytes 65568 | tf_op jit(solution)/shard_map/ppermute | solution.py:17
  14.4 1.3 %collective-permute-start.2 = (bf16[18,1,128]{2,1,0:T(2,128)(2,1)S(1)}, bf16[18,1,128]{2,1,0:T(2,128)(2,1)S(1)}, u32[]{:S(2)}, u32[]{:S(2)}) collective-permute-start(bf16[18,1,128]{2,1,0:T(2,128)(2,1)S(1)} %get-tuple-element.11), channel_id=1, source_target_pairs={{0,1},{2,3},{4,5},{6,7},{8,9},{10,11},{12,13},{14,15},{16,17},{18,... | collective-permute-start | bytes 13832 | tf_op jit(solution)/shard_map/ppermute | solution.py:15
  15.7 1.3 %collective-permute-start.3 = (bf16[18,1,128]{2,1,0:T(2,128)(2,1)S(1)}, bf16[18,1,128]{2,1,0:T(2,128)(2,1)S(1)}, u32[]{:S(2)}, u32[]{:S(2)}) collective-permute-start(bf16[18,1,128]{2,1,0:T(2,128)(2,1)S(1)} %get-tuple-element.12), channel_id=1, source_target_pairs={{1,0},{3,2},{5,4},{7,6},{9,8},{11,10},{13,12},{15,14},{17,16},{19,... | collective-permute-start | bytes 13832 | tf_op jit(solution)/shard_map/ppermute | solution.py:17
  17.0 1.2 %fusion.10 = f32[16,256,128]{2,1,0:T(8,128)S(1)} fusion(bf16[1,256,128]{2,1,0:T(8,128)(2,1)S(1)} %collective-permute-done.1, bf16[16,256,128]{2,1,0:T(8,128)(2,1)S(1)} %add_convert_fusion.3, bf16[2,9,128,128]{3,2,1,0:T(8,128)(2,1)} %param.17), kind=kOutput, calls=%fused_computation.22 | convolution fusion | flops 136445952 | bytes 3244032 | tf_op jit(solution)/shard_map/rci,io->rco/dot_general | solution.py:30
  18.2 1.2 %fusion.6 = f32[16,256,128]{2,1,0:T(8,128)S(1)} fusion(bf16[16,256,128]{2,1,0:T(8,128)(2,1)S(1)} %add_convert_fusion.3, bf16[1,256,128]{2,1,0:T(8,128)(2,1)S(1)} %collective-permute-done, bf16[2,9,128,128]{3,2,1,0:T(8,128)(2,1)} %param.17), kind=kOutput, calls=%fused_computation.18 | convolution fusion | flops 136445952 | bytes 3244032 | tf_op jit(solution)/shard_map/rci,io->rco/dot_general | solution.py:30
  20.0 1.2 %fusion.43 = f32[16,256,128]{2,1,0:T(8,128)S(1)} fusion(bf16[18,257,128]{2,1,0:T(8,128)(2,1)S(1)} %get-tuple-element.9, bf16[2,9,128,128]{3,2,1,0:T(8,128)(2,1)} %param.17), kind=kOutput, calls=%fused_computation.49 | convolution fusion | flops 134217728 | bytes 3178496 | tf_op jit(solution)/shard_map/rci,io->rco/dot_general | solution.py:30
  22.4 1.2 %fusion.51 = f32[16,256,128]{2,1,0:T(8,128)S(1)} fusion(bf16[18,257,128]{2,1,0:T(8,128)(2,1)S(1)} %get-tuple-element.9, bf16[2,9,128,128]{3,2,1,0:T(8,128)(2,1)} %param.17), kind=kOutput, calls=%fused_computation.57 | convolution fusion | flops 134217728 | bytes 3178496 | tf_op jit(solution)/shard_map/rci,io->rco/dot_general | solution.py:30
  23.5 1.2 %fusion.45 = f32[16,256,128]{2,1,0:T(8,128)S(1)} fusion(bf16[18,257,128]{2,1,0:T(8,128)(2,1)S(1)} %get-tuple-element.10, bf16[2,9,128,128]{3,2,1,0:T(8,128)(2,1)} %param.17), kind=kOutput, calls=%fused_computation.51 | convolution fusion | flops 134217728 | bytes 3178496 | tf_op jit(solution)/shard_map/rci,io->rco/dot_general | solution.py:30
  24.8 1.3 %fusion.49 = f32[16,256,128]{2,1,0:T(8,128)S(1)} fusion(bf16[18,257,128]{2,1,0:T(8,128)(2,1)S(1)} %get-tuple-element.10, bf16[2,9,128,128]{3,2,1,0:T(8,128)(2,1)} %param.17), kind=kOutput, calls=%fused_computation.55 | convolution fusion | flops 134217728 | bytes 3178496 | tf_op jit(solution)/shard_map/rci,io->rco/dot_general | solution.py:30
  26.4 2.3 %fusion.40 = f32[16,256,128]{2,1,0:T(8,128)S(1)} fusion(bf16[18,257,128]{2,1,0:T(8,128)(2,1)S(1)} %get-tuple-element.10, f32[16,256,128]{2,1,0:T(8,128)S(1)} %fusion.10, f32[16,256,128]{2,1,0:T(8,128)S(1)} %fusion.43, f32[16,256,128]{2,1,0:T(8,128)S(1)} %fusion.45, f32[16,256,128]{2,1,0:T(8,128)S(1)} %copy-done.1, f32[16,256,128]{2,1,0:T(8,128)S(1)} %fusion.47, ...), kind=kOutput, calls=%fused_computation.48 | convolution fusion | flops 142606336 | bytes 21004288 | tf_op jit(solution)/shard_map/rci,io->rco/dot_general | solution.py:30
  28.6 1.5 %reduce_sum.18 = f32[8,128,128]{2,1,0:T(8,128)S(1)} reduce(f32[8,2,128,2,128]{4,3,2,1,0:T(2,128)S(1)} %bitcast.157, f32[]{:T(128)} %constant.10.clone.1), dimensions={1,3}, to_apply=%region_0.1 | reduce | flops 393216 | bytes 2621444 | tf_op jit(solution)/shard_map/reduce_sum | solution.py:71
  30.5 3.6 %collective-permute-start.4 = (bf16[1,128,256]{2,1,0:T(8,128)(2,1)S(1)}, bf16[1,128,256]{2,1,0:T(8,128)(2,1)S(1)}, u32[]{:S(2)}, u32[]{:S(2)}) collective-permute-start(bf16[1,128,256]{2,1,0:T(8,128)(2,1)S(1)} %get-tuple-element.21), channel_id=1, source_target_pairs={{0,4},{4,8},{8,12},{1,5},{5,9},{9,13},{2,6},{6,10},{10,14},{3,7},{... | collective-permute-start | bytes 196616 | tf_op jit(solution)/shard_map/ppermute | solution.py:15
  34.1 1.3 %collective-permute-start.5 = (bf16[1,128,256]{2,1,0:T(8,128)(2,1)S(1)}, bf16[1,128,256]{2,1,0:T(8,128)(2,1)S(1)}, u32[]{:S(2)}, u32[]{:S(2)}) collective-permute-start(bf16[1,128,256]{2,1,0:T(8,128)(2,1)S(1)} %get-tuple-element.22), channel_id=1, source_target_pairs={{4,0},{8,4},{12,8},{5,1},{9,5},{13,9},{6,2},{10,6},{14,10},{7,3},{... | collective-permute-start | bytes 196616 | tf_op jit(solution)/shard_map/ppermute | solution.py:17
  35.4 1.2 %fusion.83 = f32[8,128,256]{2,1,0:T(8,128)S(1)} fusion(bf16[8,128,256]{2,1,0:T(8,128)(2,1)S(1)} %convolution_convert_fusion, bf16[9,256,256]{2,1,0:T(8,128)(2,1)} %param.18), kind=kOutput, calls=%fused_computation.89 | convolution fusion | flops 134217728 | bytes 1703936 | tf_op jit(solution)/shard_map/rci,io->rco/dot_general | solution.py:30
  36.6 4.2 %collective-permute-done.5 = bf16[1,128,256]{2,1,0:T(8,128)(2,1)S(1)} collective-permute-done((bf16[1,128,256]{2,1,0:T(8,128)(2,1)S(1)}, bf16[1,128,256]{2,1,0:T(8,128)(2,1)S(1)}, u32[]{:S(2)}, u32[]{:S(2)}) %collective-permute-start.5) | collective-permute-done | bytes 65568 | tf_op jit(solution)/shard_map/ppermute | solution.py:17
  40.8 1.9 %collective-permute-start.6 = (bf16[10,1,256]{2,1,0:T(2,128)(2,1)S(1)}, bf16[10,1,256]{2,1,0:T(2,128)(2,1)S(1)}, u32[]{:S(2)}, u32[]{:S(2)}) collective-permute-start(bf16[10,1,256]{2,1,0:T(2,128)(2,1)S(1)} %get-tuple-element.19), channel_id=1, source_target_pairs={{0,1},{2,3},{4,5},{6,7},{8,9},{10,11},{12,13},{14,15},{16,17},{18,... | collective-permute-start | bytes 15368 | tf_op jit(solution)/shard_map/ppermute | solution.py:15
  42.7 1.3 %collective-permute-start.7 = (bf16[10,1,256]{2,1,0:T(2,128)(2,1)S(1)}, bf16[10,1,256]{2,1,0:T(2,128)(2,1)S(1)}, u32[]{:S(2)}, u32[]{:S(2)}) collective-permute-start(bf16[10,1,256]{2,1,0:T(2,128)(2,1)S(1)} %get-tuple-element.20), channel_id=1, source_target_pairs={{1,0},{3,2},{5,4},{7,6},{9,8},{11,10},{13,12},{15,14},{17,16},{19,... | collective-permute-start | bytes 15368 | tf_op jit(solution)/shard_map/ppermute | solution.py:17
  44.0 1.3 %fusion.61 = f32[8,128,256]{2,1,0:T(8,128)} fusion(bf16[1,128,256]{2,1,0:T(8,128)(2,1)S(1)} %collective-permute-done.5, bf16[8,128,256]{2,1,0:T(8,128)(2,1)S(1)} %convolution_convert_fusion, bf16[9,256,256]{2,1,0:T(8,128)(2,1)S(1)} %copy-done.3), kind=kOutput, calls=%fused_computation.68 | convolution fusion | flops 135397376 | bytes 1769472 | tf_op jit(solution)/shard_map/rci,io->rco/dot_general | solution.py:30
  46.0 1.3 %fusion.67 = f32[8,128,256]{2,1,0:T(8,128)} fusion(bf16[10,129,256]{2,1,0:T(8,128)(2,1)S(1)} %get-tuple-element.17, bf16[9,256,256]{2,1,0:T(8,128)(2,1)S(1)} %copy-done.3), kind=kOutput, calls=%fused_computation.74 | convolution fusion | flops 134217728 | bytes 1703936 | tf_op jit(solution)/shard_map/rci,io->rco/dot_general | solution.py:30
  47.6 1.3 %fusion.65 = f32[8,128,256]{2,1,0:T(8,128)} fusion(bf16[10,129,256]{2,1,0:T(8,128)(2,1)S(1)} %get-tuple-element.18, bf16[9,256,256]{2,1,0:T(8,128)(2,1)S(1)} %copy-done.3), kind=kOutput, calls=%fused_computation.72 | convolution fusion | flops 134217728 | bytes 1703936 | tf_op jit(solution)/shard_map/rci,io->rco/dot_general | solution.py:30
  49.2 1.3 %fusion.5 = f32[8,128,256]{2,1,0:T(8,128)} fusion(f32[8,128,256]{2,1,0:T(8,128)S(1)} %fusion.83, f32[8,128,256]{2,1,0:T(8,128)S(1)} %fusion.71, f32[8,128,256]{2,1,0:T(8,128)S(1)} %fusion.73, f32[8,128,256]{2,1,0:T(8,128)S(1)} %fusion.57, bf16[10,129,256]{2,1,0:T(8,128)(2,1)S(1)} %get-tuple-element.17, bf16[9,256,256]{2,1,0:T(8,128)(2,1)S(1)} %copy-done.3), kind=kOutput, calls=%fused_computation.12 | convolution fusion | flops 135266304 | bytes 5898240 | tf_op jit(solution)/shard_map/rci,io->rco/dot_general | solution.py:30
  50.6 3.9 %fusion.53 = f32[8,128,128]{2,1,0:T(8,128)} fusion(f32[8,128,256]{2,1,0:T(8,128)} %fusion.65, f32[8,128,256]{2,1,0:T(8,128)} %fusion.61, f32[8,128,256]{2,1,0:T(8,128)} %fusion.67, f32[8,128,256]{2,1,0:T(8,128)} %fusion.5, bf16[8,128,256]{2,1,0:T(8,128)(2,1)S(1)} %convolution_convert_fusion, bf16[10,129,256]{2,1,0:T(8,128)(2,1)} %copy-done.2, ...), kind=kOutput, calls=%fused_computation.60 | convolution fusion | flops 204210176 | bytes 5963776 | tf_op jit(solution)/shard_map/rci,io->rco/dot_general | solution.py:82
  56.7 3.5 %collective-permute-start.8 = (bf16[1,256,128]{2,1,0:T(8,128)(2,1)S(1)}, bf16[1,256,128]{2,1,0:T(8,128)(2,1)S(1)}, u32[]{:S(2)}, u32[]{:S(2)}) collective-permute-start(bf16[1,256,128]{2,1,0:T(8,128)(2,1)S(1)} %get-tuple-element.13), channel_id=1, source_target_pairs={{0,4},{4,8},{8,12},{1,5},{5,9},{9,13},{2,6},{6,10},{10,14},{3,7},{... | collective-permute-start | bytes 196616 | tf_op jit(solution)/shard_map/ppermute | solution.py:15
  60.2 1.3 %collective-permute-start.9 = (bf16[1,256,128]{2,1,0:T(8,128)(2,1)S(1)}, bf16[1,256,128]{2,1,0:T(8,128)(2,1)S(1)}, u32[]{:S(2)}, u32[]{:S(2)}) collective-permute-start(bf16[1,256,128]{2,1,0:T(8,128)(2,1)S(1)} %get-tuple-element.14), channel_id=1, source_target_pairs={{4,0},{8,4},{12,8},{5,1},{9,5},{13,9},{6,2},{10,6},{14,10},{7,3},{... | collective-permute-start | bytes 196616 | tf_op jit(solution)/shard_map/ppermute | solution.py:17
  62.6 4.1 %collective-permute-done.9 = bf16[1,256,128]{2,1,0:T(8,128)(2,1)S(1)} collective-permute-done((bf16[1,256,128]{2,1,0:T(8,128)(2,1)S(1)}, bf16[1,256,128]{2,1,0:T(8,128)(2,1)S(1)}, u32[]{:S(2)}, u32[]{:S(2)}) %collective-permute-start.9) | collective-permute-done | bytes 65568 | tf_op jit(solution)/shard_map/ppermute | solution.py:17
  66.7 1.7 %collective-permute-start.10 = (bf16[18,1,128]{2,1,0:T(2,128)(2,1)S(1)}, bf16[18,1,128]{2,1,0:T(2,128)(2,1)S(1)}, u32[]{:S(2)}, u32[]{:S(2)}) collective-permute-start(bf16[18,1,128]{2,1,0:T(2,128)(2,1)S(1)} %get-tuple-element.7), channel_id=1, source_target_pairs={{0,1},{2,3},{4,5},{6,7},{8,9},{10,11},{12,13},{14,15},{16,17},{18,... | collective-permute-start | bytes 13832 | tf_op jit(solution)/shard_map/ppermute | solution.py:15
  68.5 1.5 %collective-permute-start.11 = (bf16[18,1,128]{2,1,0:T(2,128)(2,1)S(1)}, bf16[18,1,128]{2,1,0:T(2,128)(2,1)S(1)}, u32[]{:S(2)}, u32[]{:S(2)}) collective-permute-start(bf16[18,1,128]{2,1,0:T(2,128)(2,1)S(1)} %get-tuple-element.8), channel_id=1, source_target_pairs={{1,0},{3,2},{5,4},{7,6},{9,8},{11,10},{13,12},{15,14},{17,16},{19,... | collective-permute-start | bytes 13832 | tf_op jit(solution)/shard_map/ppermute | solution.py:17
  74.3 1.9 %multiply_reduce_fusion = f32[16,256]{1,0:T(8,128)S(1)} fusion(f32[128]{0:T(128)S(1)} %convert_element_type.56, bf16[18,257,128]{2,1,0:T(8,128)(2,1)S(1)} %get-tuple-element.6, f32[16,256,128]{2,1,0:T(8,128)S(1)} %fusion.18, f32[16,256,128]{2,1,0:T(8,128)S(1)} %fusion.26, f32[16,256,128]{2,1,0:T(8,128)S(1)} %fusion.28, f32[16,256,128]{2,1,0:T(8,128)S(1)} %fusion.105, ...), kind=kOutput, calls=%fused_computation | convolution fusion | flops 143650816 | bytes 18924032 | tf_op jit(solution)/shard_map/rci,io->rco/dot_general | solution.py:30
  (55 shorter events, 12.7 us)
Async XLA Ops:
  0.0 30.1 %copy-start = (bf16[128,256]{1,0:T(8,128)(2,1)S(1)}, bf16[128,256]{1,0:T(8,128)(2,1)}, u32[]{:S(2)}) copy-start(bf16[128,256]{1,0:T(8,128)(2,1)} %param.19) | copy-start | bytes 196612
  3.2 9.6 %copy-start.8 = (bf16[128]{0:T(256)(128)(2,1)S(1)}, bf16[128]{0:T(256)(128)(2,1)}, u32[]{:S(2)}) copy-start(bf16[128]{0:T(256)(128)(2,1)} %param.21) | copy-start | bytes 772
  3.2 9.6 %collective-permute-start = (bf16[1,256,128]{2,1,0:T(8,128)(2,1)S(1)}, bf16[1,256,128]{2,1,0:T(8,128)(2,1)S(1)}, u32[]{:S(2)}, u32[]{:S(2)}) collective-permute-start(bf16[1,256,128]{2,1,0:T(8,128)(2,1)S(1)} %get-tuple-element.15), channel_id=1, source_target_pairs={{0,4},{4,8},{8,12},{1,5},{5,9},{9,13},{2,6},{6,10},{10,14},{3,7},{... | collective-permute-start | bytes 196616 | tf_op jit(solution)/shard_map/ppermute | solution.py:15
  8.2 6.2 %collective-permute-start.1 = (bf16[1,256,128]{2,1,0:T(8,128)(2,1)S(1)}, bf16[1,256,128]{2,1,0:T(8,128)(2,1)S(1)}, u32[]{:S(2)}, u32[]{:S(2)}) collective-permute-start(bf16[1,256,128]{2,1,0:T(8,128)(2,1)S(1)} %get-tuple-element.16), channel_id=1, source_target_pairs={{4,0},{8,4},{12,8},{5,1},{9,5},{13,9},{6,2},{10,6},{14,10},{7,3},{... | collective-permute-start | bytes 196616 | tf_op jit(solution)/shard_map/ppermute | solution.py:17
  14.4 5.0 %collective-permute-start.2 = (bf16[18,1,128]{2,1,0:T(2,128)(2,1)S(1)}, bf16[18,1,128]{2,1,0:T(2,128)(2,1)S(1)}, u32[]{:S(2)}, u32[]{:S(2)}) collective-permute-start(bf16[18,1,128]{2,1,0:T(2,128)(2,1)S(1)} %get-tuple-element.11), channel_id=1, source_target_pairs={{0,1},{2,3},{4,5},{6,7},{8,9},{10,11},{12,13},{14,15},{16,17},{18,... | collective-permute-start | bytes 13832 | tf_op jit(solution)/shard_map/ppermute | solution.py:15
  15.7 3.7 %collective-permute-start.3 = (bf16[18,1,128]{2,1,0:T(2,128)(2,1)S(1)}, bf16[18,1,128]{2,1,0:T(2,128)(2,1)S(1)}, u32[]{:S(2)}, u32[]{:S(2)}) collective-permute-start(bf16[18,1,128]{2,1,0:T(2,128)(2,1)S(1)} %get-tuple-element.12), channel_id=1, source_target_pairs={{1,0},{3,2},{5,4},{7,6},{9,8},{11,10},{13,12},{15,14},{17,16},{19,... | collective-permute-start | bytes 13832 | tf_op jit(solution)/shard_map/ppermute | solution.py:17
  24.7 1.6 %copy-start.1 = (f32[16,256,128]{2,1,0:T(8,128)S(1)}, f32[16,256,128]{2,1,0:T(8,128)}, u32[]{:S(2)}) copy-start(f32[16,256,128]{2,1,0:T(8,128)} %fusion.115) | copy-start | bytes 6291460
  30.2 13.9 %copy-start.3 = (bf16[9,256,256]{2,1,0:T(8,128)(2,1)S(1)}, bf16[9,256,256]{2,1,0:T(8,128)(2,1)}, u32[]{:S(2)}) copy-start(bf16[9,256,256]{2,1,0:T(8,128)(2,1)} %param.18) | copy-start | bytes 3538948
  30.5 6.1 %collective-permute-start.4 = (bf16[1,128,256]{2,1,0:T(8,128)(2,1)S(1)}, bf16[1,128,256]{2,1,0:T(8,128)(2,1)S(1)}, u32[]{:S(2)}, u32[]{:S(2)}) collective-permute-start(bf16[1,128,256]{2,1,0:T(8,128)(2,1)S(1)} %get-tuple-element.21), channel_id=1, source_target_pairs={{0,4},{4,8},{8,12},{1,5},{5,9},{9,13},{2,6},{6,10},{10,14},{3,7},{... | collective-permute-start | bytes 196616 | tf_op jit(solution)/shard_map/ppermute | solution.py:15
  34.1 6.7 %collective-permute-start.5 = (bf16[1,128,256]{2,1,0:T(8,128)(2,1)S(1)}, bf16[1,128,256]{2,1,0:T(8,128)(2,1)S(1)}, u32[]{:S(2)}, u32[]{:S(2)}) collective-permute-start(bf16[1,128,256]{2,1,0:T(8,128)(2,1)S(1)} %get-tuple-element.22), channel_id=1, source_target_pairs={{4,0},{8,4},{12,8},{5,1},{9,5},{13,9},{6,2},{10,6},{14,10},{7,3},{... | collective-permute-start | bytes 196616 | tf_op jit(solution)/shard_map/ppermute | solution.py:17
  40.8 4.8 %collective-permute-start.6 = (bf16[10,1,256]{2,1,0:T(2,128)(2,1)S(1)}, bf16[10,1,256]{2,1,0:T(2,128)(2,1)S(1)}, u32[]{:S(2)}, u32[]{:S(2)}) collective-permute-start(bf16[10,1,256]{2,1,0:T(2,128)(2,1)S(1)} %get-tuple-element.19), channel_id=1, source_target_pairs={{0,1},{2,3},{4,5},{6,7},{8,9},{10,11},{12,13},{14,15},{16,17},{18,... | collective-permute-start | bytes 15368 | tf_op jit(solution)/shard_map/ppermute | solution.py:15
  42.7 3.1 %collective-permute-start.7 = (bf16[10,1,256]{2,1,0:T(2,128)(2,1)S(1)}, bf16[10,1,256]{2,1,0:T(2,128)(2,1)S(1)}, u32[]{:S(2)}, u32[]{:S(2)}) collective-permute-start(bf16[10,1,256]{2,1,0:T(2,128)(2,1)S(1)} %get-tuple-element.20), channel_id=1, source_target_pairs={{1,0},{3,2},{5,4},{7,6},{9,8},{11,10},{13,12},{15,14},{17,16},{19,... | collective-permute-start | bytes 15368 | tf_op jit(solution)/shard_map/ppermute | solution.py:17
  46.0 2.9 %copy-start.2 = (bf16[10,129,256]{2,1,0:T(8,128)(2,1)}, bf16[10,129,256]{2,1,0:T(8,128)(2,1)S(1)}, u32[]{:S(2)}) copy-start(bf16[10,129,256]{2,1,0:T(8,128)(2,1)S(1)} %get-tuple-element.18) | copy-start | bytes 1981444
  49.2 1.3 %copy-start.7 = (bf16[256,128]{1,0:T(8,128)(2,1)S(1)}, bf16[256,128]{1,0:T(8,128)(2,1)}, u32[]{:S(2)}) copy-start(bf16[256,128]{1,0:T(8,128)(2,1)} %param.20) | copy-start | bytes 196612
  56.4 5.1 %copy-start.4 = (bf16[2,9,128,128]{3,2,1,0:T(8,128)(2,1)S(1)}, bf16[2,9,128,128]{3,2,1,0:T(8,128)(2,1)}, u32[]{:S(2)}) copy-start(bf16[2,9,128,128]{3,2,1,0:T(8,128)(2,1)} %param.17) | copy-start | bytes 1769476
  56.7 5.9 %collective-permute-start.8 = (bf16[1,256,128]{2,1,0:T(8,128)(2,1)S(1)}, bf16[1,256,128]{2,1,0:T(8,128)(2,1)S(1)}, u32[]{:S(2)}, u32[]{:S(2)}) collective-permute-start(bf16[1,256,128]{2,1,0:T(8,128)(2,1)S(1)} %get-tuple-element.13), channel_id=1, source_target_pairs={{0,4},{4,8},{8,12},{1,5},{5,9},{9,13},{2,6},{6,10},{10,14},{3,7},{... | collective-permute-start | bytes 196616 | tf_op jit(solution)/shard_map/ppermute | solution.py:15
  60.2 6.6 %collective-permute-start.9 = (bf16[1,256,128]{2,1,0:T(8,128)(2,1)S(1)}, bf16[1,256,128]{2,1,0:T(8,128)(2,1)S(1)}, u32[]{:S(2)}, u32[]{:S(2)}) collective-permute-start(bf16[1,256,128]{2,1,0:T(8,128)(2,1)S(1)} %get-tuple-element.14), channel_id=1, source_target_pairs={{4,0},{8,4},{12,8},{5,1},{9,5},{13,9},{6,2},{10,6},{14,10},{7,3},{... | collective-permute-start | bytes 196616 | tf_op jit(solution)/shard_map/ppermute | solution.py:17
  66.7 4.0 %collective-permute-start.10 = (bf16[18,1,128]{2,1,0:T(2,128)(2,1)S(1)}, bf16[18,1,128]{2,1,0:T(2,128)(2,1)S(1)}, u32[]{:S(2)}, u32[]{:S(2)}) collective-permute-start(bf16[18,1,128]{2,1,0:T(2,128)(2,1)S(1)} %get-tuple-element.7), channel_id=1, source_target_pairs={{0,1},{2,3},{4,5},{6,7},{8,9},{10,11},{12,13},{14,15},{16,17},{18,... | collective-permute-start | bytes 13832 | tf_op jit(solution)/shard_map/ppermute | solution.py:15
  68.5 3.1 %collective-permute-start.11 = (bf16[18,1,128]{2,1,0:T(2,128)(2,1)S(1)}, bf16[18,1,128]{2,1,0:T(2,128)(2,1)S(1)}, u32[]{:S(2)}, u32[]{:S(2)}) collective-permute-start(bf16[18,1,128]{2,1,0:T(2,128)(2,1)S(1)} %get-tuple-element.8), channel_id=1, source_target_pairs={{1,0},{3,2},{5,4},{7,6},{9,8},{11,10},{13,12},{15,14},{17,16},{19,... | collective-permute-start | bytes 13832 | tf_op jit(solution)/shard_map/ppermute | solution.py:17
  74.3 2.0 %copy-start.5 = (f32[16,256]{1,0:T(8,128)S(1)}, f32[16,256]{1,0:T(8,128)}, u32[]{:S(2)}) copy-start(f32[16,256]{1,0:T(8,128)} %param.11) | copy-start | bytes 49156
  74.3 1.9 %copy-start.6 = (f32[16,256]{1,0:T(8,128)S(1)}, f32[16,256]{1,0:T(8,128)}, u32[]{:S(2)}) copy-start(f32[16,256]{1,0:T(8,128)} %param.12) | copy-start | bytes 49156
where the time goes:
time: 78 us; the launch traced here: 76.9 us
  matrix products  30 us (38%)
  starting transfers between devices  24.9 us (32%)
  waiting for transfers between devices  11.5 us (15%)
  other arithmetic  6.41 us (8%)
  local copies, waits for them, and re-layouts  2.21 us (3%)
  between operations  1.92 us (2%)
    dot_general x26, matrix products, tap_sum(): jnp.einsum('rci,io->rco', window, kernel[kernel_tap], preferred_element_t...  25.8 us
    ppermute x6, starting transfers between devices, padded_2(): lax.ppermute(tail, axis, [(i, (i + 1) % count) for i in range(ends)])  16.9 us
    ppermute x6, waiting for transfers between devices, padded_2(): lax.ppermute(head, axis, [((i + 1) % count, i) for i in range(ends)])  10.8 us
    ppermute x6, starting transfers between devices, padded_2(): lax.ppermute(head, axis, [((i + 1) % count, i) for i in range(ends)])  7.93 us
    dot_general x1, matrix products, per_device(): jnp.einsum('rci,io->rco', coarse_out, up_proj, preferred_element_type=jnp...  3.93 us
    broadcast_in_dim x2, local copies, waits for them, and re-layouts, per_device(): lifted = jnp.repeat(jnp.repeat(lifted, 2, axis=0), 2, axis=1)  1.87 us
    convert_element_type x1, other arithmetic, per_device(): hidden0 = (cond_features.astype(jnp.float32) + (scale_in * noisy_field)[:...  1.76 us
  transfers between devices with their start and end apart: 12, of which 6 were waited for; matrix products, arithmetic and copies ran while one was open for 12% of the time, Pallas kernels for 0%

commit v1 on v0

v1 whole, which is shorter than its diff:
```python
import functools

import jax
import jax.numpy as jnp
from jax import lax
from jax.experimental import pallas as pl
from jax.experimental.pallas import tpu as pltpu
from jax.sharding import PartitionSpec as P

F32 = jnp.float32
BF16 = jnp.bfloat16
HALO = 5
EDGE = 16
PER = EDGE // 2


def silu(v):
    half = 0.5 * v
    return half + half * jnp.tanh(half)


def column_mask(ring, own, index, count):
    at = lax.broadcasted_iota(jnp.int32, (ring, 128), 0)
    right = jnp.where(index < count - 1, 1, 0)
    left = jnp.where(index > 0, 1, 0)
    inside = jnp.where(at < own, 1, jnp.where(at < own + PER, right, left))
    return inside.astype(F32)


def embed_kernel(now_ref, cond_ref, noisy_ref, proj_ref, left_ref, right_ref, out_ref, wide, edge, *, sub, count):
    rows, cols, _ = cond_ref.shape
    index = lax.axis_index(sub)
    level = jnp.full((1, 128), now_ref[0], F32)
    scale_in = 1.0 / jnp.sqrt(level * level + 1.0)
    noisy = noisy_ref[...] * scale_in[:, :1]
    turned = jnp.transpose(noisy)
    proj = proj_ref[...]
    keep_left = jnp.where(index > 0, 1.0, 0.0).astype(F32)
    keep_right = jnp.where(index < count - 1, 1.0, 0.0).astype(F32)
    for r in range(rows):
        wide[r % 2] = cond_ref[r].astype(F32) + turned[:, r : r + 1] * proj
        edge[r % 2, :EDGE] = left_ref[r].astype(F32) * keep_left
        edge[r % 2, EDGE:] = right_ref[r].astype(F32) * keep_right
        for q in range(2):
            main = wide[r % 2, pl.ds(q, cols // 2, stride=2), :]
            lt = edge[r % 2, pl.ds(q, PER, stride=2), :]
            rt = edge[r % 2, pl.ds(EDGE + q, PER, stride=2), :]
            out_ref[r, q] = jnp.concatenate([main, rt, lt], axis=0).astype(BF16)


def step_kernel(
    now_ref, next_ref, own_ref, top_ref, bot_ref, fine_ref, coarse_ref, down_ref, up_ref, outp_ref,
    noisy_ref, noise_ref, out_ref,
    x_ref, w_ref, h1_ref, pool_ref, ci_ref, co_ref, h2_ref, h3_ref, flat_ref,
    *, patch, patches, sub, subs,
):
    rows, _, ring, c1 = own_ref.shape
    own = out_ref.shape[1] // 2
    c2 = down_ref.shape[1]
    p = lax.axis_index(patch)
    s = lax.axis_index(sub)
    inside = column_mask(ring, own, s, subs)
    above = jnp.where(p > 0, 1.0, 0.0).astype(F32)
    below = jnp.where(p < patches - 1, 1.0, 0.0).astype(F32)

    def row_mask(r, extent):
        if r < 0:
            return inside * above
        if r >= extent:
            return inside * below
        return inside

    for layer in range(2):
        for b in range(3):
            for d in range(4):
                at = (b * 4 + d) * c1
                for o in range(2):
                    a = d - o
                    block = fine_ref[layer, a * 3 + b] if 0 <= a <= 2 else jnp.zeros((c1, c1), BF16)
                    w_ref[layer, at : at + c1, o * c1 : (o + 1) * c1] = block

    def put_planes(ref, at, even, odd):
        ref[at, 0] = even.astype(BF16)
        ref[at, 1] = odd.astype(BF16)
        ref[at, 2] = pltpu.roll(odd, 1, 0).astype(BF16)
        ref[at, 3] = pltpu.roll(even, ring - 1, 0).astype(BF16)

    for r in range(-HALO, rows + HALO):
        src, at = (top_ref, r + HALO) if r < 0 else (own_ref, r) if r < rows else (bot_ref, r - rows)
        put_planes(x_ref, r + HALO, src[at, 0].astype(F32), src[at, 1].astype(F32))

    def conv_pair(ref, at, layer):
        parts = []
        for planes in ((2, 0, 1), (0, 1, 3)):
            parts.append(jnp.concatenate([ref[at + d, k] for k in planes for d in range(4)], axis=1))
        lhs = jnp.concatenate(parts, axis=0)
        return jnp.dot(lhs, w_ref[layer], preferred_element_type=F32)

    half = rows // 2
    for i in range(-2, half + 2):
        acc = conv_pair(x_ref, 2 * i - 1 + HALO, 0)
        total = None
        for o in range(2):
            for q in range(2):
                v = acc[q * ring : (q + 1) * ring, o * c1 : (o + 1) * c1]
                h = (x_ref[2 * i + o + HALO, q].astype(F32) + silu(v)).astype(BF16)
                if -1 <= 2 * i + o <= rows:
                    h1_ref[2 * i + o + 1, q] = h
                total = h.astype(F32) if total is None else total + h.astype(F32)
        pool_ref[(i + 2) * ring : (i + 3) * ring] = (total * 0.25).astype(BF16)

    for i in range(-2, half + 2):
        ci = jnp.dot(pool_ref[(i + 2) * ring : (i + 3) * ring], down_ref[...], preferred_element_type=F32)
        mask = row_mask(i, half)
        ci = ci * jnp.concatenate([mask] * (c2 // 128), axis=1)
        ci_ref[i + 2, 0] = pltpu.roll(ci, 1, 0).astype(BF16)
        ci_ref[i + 2, 1] = ci.astype(BF16)
        ci_ref[i + 2, 2] = pltpu.roll(ci, ring - 1, 0).astype(BF16)
    for i in range(-1, half + 1):
        lhs = jnp.concatenate([ci_ref[i + 1 + a, b] for a in range(3) for b in range(3)], axis=1)
        v = jnp.dot(lhs, coarse_ref[...], preferred_element_type=F32)
        co = (ci_ref[i + 2, 1].astype(F32) + silu(v)).astype(BF16)
        co_ref[(i + 1) * ring : (i + 2) * ring] = co

    for i in range(-1, half + 1):
        lifted = jnp.dot(co_ref[(i + 1) * ring : (i + 2) * ring], up_ref[...], preferred_element_type=F32)
        for o in range(2):
            r = 2 * i + o
            if -1 <= r <= rows:
                mask = row_mask(r, rows)
                put_planes(
                    h2_ref, r + 1,
                    (h1_ref[r + 1, 0].astype(F32) + lifted) * mask,
                    (h1_ref[r + 1, 1].astype(F32) + lifted) * mask,
                )

    for i in range(half):
        acc = conv_pair(h2_ref, 2 * i, 1)
        for o in range(2):
            for q in range(2):
                v = acc[q * ring : (q + 1) * ring, o * c1 : (o + 1) * c1]
                h = h2_ref[2 * i + o + 1, q].astype(F32) + silu(v)
                h3_ref[q, 2 * i + o] = h[:own].astype(BF16)

    spread = jnp.transpose(jnp.broadcast_to(outp_ref[...].astype(F32), (128, c1)))
    lane = lax.broadcasted_iota(jnp.int32, (c1, 128), 1)
    pick = jnp.concatenate([jnp.where(lane == r, spread, 0.0).astype(BF16) for r in range(rows)], axis=0)
    for q in range(2):
        lhs = jnp.concatenate([h3_ref[q, r] for r in range(rows)], axis=1)
        flat_ref[pl.ds(q, own, stride=2), :] = jnp.dot(lhs, pick, preferred_element_type=F32)
    network = jnp.transpose(flat_ref[...])[:rows]

    level = jnp.full((1, 128), now_ref[0], F32)
    after = jnp.full((1, 128), next_ref[0], F32)
    scale_in = 1.0 / jnp.sqrt(level * level + 1.0)
    scale_skip = (1.0 / (level * level + 1.0))[:, :1]
    scale_out = (level * scale_in)[:, :1]
    ratio = (after / level)[:, :1]
    spread_by = jnp.sqrt(level * level - after * after)[:, :1]
    noisy = noisy_ref[...]
    denoised = scale_skip * noisy + scale_out * network
    out_ref[...] = denoised + ratio * (noisy - denoised) + spread_by * noise_ref[...]


def per_device(
    sizes,
    noisy_field, noise_draw, cond_features, sigma_now, sigma_next, field_proj,
    fine_kernels, coarse_kernel, down_proj, up_proj, out_proj,
):
    rows, cols, c1 = cond_features.shape
    c2 = down_proj.shape[1]
    patches, subs = sizes["patch"], sizes["sub"]
    own = cols // 2
    ring = own + EDGE
    half = rows // 2
    smem = pl.BlockSpec(memory_space=pltpu.SMEM)
    vmem = pl.BlockSpec(memory_space=pltpu.VMEM)
    level = sigma_now[0]
    scale_in = 1.0 / jnp.sqrt(level * level + 1.0)

    def edge_at(start):
        cond = lax.dynamic_slice_in_dim(cond_features, start, EDGE, 1)
        noisy = lax.dynamic_slice_in_dim(noisy_field, start, EDGE, 1)
        return (cond.astype(F32) + (scale_in * noisy)[:, :, None] * field_proj).astype(BF16)

    if subs == 2:
        start = jnp.where(lax.axis_index("sub") == 0, cols - EDGE, 0)
        left = right = lax.ppermute(edge_at(start), "sub", [(0, 1), (1, 0)])
    else:
        left = lax.ppermute(edge_at(cols - EDGE), "sub", [(i, i + 1) for i in range(subs - 1)])
        right = lax.ppermute(edge_at(0), "sub", [(i + 1, i) for i in range(subs - 1)])

    mine = pl.pallas_call(
        functools.partial(embed_kernel, sub="sub", count=subs),
        out_shape=jax.ShapeDtypeStruct((rows, 2, ring, c1), BF16),
        in_specs=[smem] + [vmem] * 5,
        out_specs=vmem,
        scratch_shapes=[pltpu.VMEM((2, cols, c1), F32), pltpu.VMEM((2, 2 * EDGE, c1), F32)],
        name="embed",
    )(sigma_now, cond_features, noisy_field, field_proj[None], left, right)

    top = lax.ppermute(mine[rows - HALO :], "patch", [(i, i + 1) for i in range(patches - 1)])
    bot = lax.ppermute(mine[:HALO], "patch", [(i + 1, i) for i in range(patches - 1)])

    return pl.pallas_call(
        functools.partial(step_kernel, patch="patch", patches=patches, sub="sub", subs=subs),
        out_shape=jax.ShapeDtypeStruct((rows, cols), F32),
        in_specs=[smem, smem] + [vmem] * 10,
        out_specs=vmem,
        scratch_shapes=[
            pltpu.VMEM((rows + 2 * HALO, 4, ring, c1), BF16),
            pltpu.VMEM((2, 12 * c1, 2 * c1), BF16),
            pltpu.VMEM((rows + 2, 2, ring, c1), BF16),
            pltpu.VMEM(((half + 4) * ring, c1), BF16),
            pltpu.VMEM((half + 4, 3, ring, c2), BF16),
            pltpu.VMEM(((half + 2) * ring, c2), BF16),
            pltpu.VMEM((rows + 2, 4, ring, c1), BF16),
            pltpu.VMEM((2, rows, own, c1), BF16),
            pltpu.VMEM((cols, 128), F32),
        ],
        name="step",
    )(
        sigma_now, sigma_next, mine, top, bot, fine_kernels, coarse_kernel.reshape(9 * c2, c2),
        down_proj, up_proj, out_proj[None], noisy_field, noise_draw,
    )


def solution(mesh):
    return jax.shard_map(
        functools.partial(per_device, dict(mesh.shape)),
        mesh=mesh,
        in_specs=(
            P(("groups", "patch"), "sub"),
            P(("groups", "patch"), "sub"),
            P(("groups", "patch"), "sub", None),
            P(),
            P(),
            P(),
            P(),
            P(),
            P(),
            P(),
            P(),
        ),
        out_specs=P(("groups", "patch"), "sub"),
        check_vma=False,
    )
```

time: 78 us -> 38.3 us (0.49); the launches traced: 76.9 us -> 38 us
  matrix products: 30 us -> 0 us
  starting transfers between devices: 24.9 us -> 6.69 us
  Pallas kernels: 0 us -> 14.5 us
  other arithmetic: 6.41 us -> 1.73 us
    dot_general x28 -> x0, matrix products: 30 us -> none  [the longest x26 25.8 us: tap_sum(): jnp.einsum('rci,io->rco', window, kernel[kernel_tap], preferred_element_t...]
    ppermute x12 -> x3, starting transfers between devices: 24.9 us -> 6.69 us  [the longest x1 4.84 us: per_device(): lax.ppermute(mine[rows - HALO:], 'patch', [(i, i + 1) for i in range(patc...]
    pallas_call x0 -> x2, Pallas kernels: none -> 14.5 us  [the longest x1 11.3 us: per_device(): pl.pallas_call(functools.partial(step_kernel, patch='patch', patches=patc...]
    broadcast_in_dim x2 -> x0, local copies, waits for them, and re-layouts: 1.87 us -> none  [per_device(): lifted = jnp.repeat(jnp.repeat(lifted, 2, axis=0), 2, axis=1)]
    reduce_sum x1 -> x0, other arithmetic: 1.51 us -> none  [per_device(): pooled = hidden1.astype(jnp.float32).reshape(height // 2, 2, breadth // 2...]
    concatenate x3 -> x0, other arithmetic: 1.48 us -> none  [padded_2(): jnp.concatenate([lax.ppermute(tail, axis, [(i, (i + 1) % count) for i in...]
    slice x3 -> x1, local copies, waits for them, and re-layouts: 0.03 us -> 1.15 us  [per_device(): mine[:HALO]]
    convert_element_type x3 -> x1, other arithmetic: 2.03 us -> 0.96 us  [edge_at(): (cond.astype(F32) + (scale_in * noisy)[:, :, None] * field_proj).astype(B...]
  transfers between devices with their start and end apart: 12 -> 3, of which waited for: 6 -> 3; matrix products, arithmetic and copies ran while one was open for 12% -> 0% of each run, Pallas kernels for 0% -> 0%
where the time goes in v1:
time: 38.3 us; the launch traced here: 38 us
  Pallas kernels  14.5 us (38%)
  waiting for transfers between devices  11.2 us (29%)
  starting transfers between devices  6.69 us (17%)
  local copies, waits for them, and re-layouts  2.5 us (7%)
  other arithmetic  1.73 us (5%)
  between operations  1.38 us (4%)
    pallas_call x1, Pallas kernels, per_device(): pl.pallas_call(functools.partial(step_kernel, patch='patch', patches=patc...  11.3 us
    ppermute x1, waiting for transfers between devices, per_device(): lax.ppermute(mine[rows - HALO:], 'patch', [(i, i + 1) for i in range(patc...  6.18 us
    ppermute x1, starting transfers between devices, per_device(): lax.ppermute(mine[rows - HALO:], 'patch', [(i, i + 1) for i in range(patc...  4.84 us
    ppermute x1, waiting for transfers between devices, per_device(): lax.ppermute(mine[:HALO], 'patch', [(i + 1, i) for i in range(patches - 1)])  4.13 us
    pallas_call x1, Pallas kernels, per_device(): pl.pallas_call(functools.partial(embed_kernel, sub='sub', count=subs), ou...  3.24 us
    unnamed x6, local copies, waits for them, and re-layouts  1.36 us
    ppermute x1, starting transfers between devices, per_device(): lax.ppermute(mine[:HALO], 'patch', [(i + 1, i) for i in range(patches - 1)])  1.29 us
    slice x1, local copies, waits for them, and re-layouts, per_device(): mine[:HALO]  1.15 us
  transfers between devices with their start and end apart: 3, of which 3 were waited for; matrix products, arithmetic and copies ran while one was open for 0% of the time, Pallas kernels for 0%

profile of v1, /device:TPU:0, one launch (start us, length us, event | category | flops | bytes accessed | tf_op | source)
XLA Modules:
  0.0 38.0 jit_solution(16573652412042133197)
XLA Ops:
  0.7 0.8 %dynamic-slice_multiply_fusion = f32[16,16]{1,0:T(8,128)S(1)} fusion(f32[16,256]{1,0:T(8,128)} %noisy_ref.3, s32[]{:T(128)S(6)} %select_n.6, f32[]{:T(128)} %bitcast.1), kind=kLoop, calls=%fused_computation.1 | loop fusion | flops 256 | bytes 2056 | tf_op jit(solution)/shard_map/mul | solution.py:184
  1.5 1.0 %add_convert_fusion = bf16[16,16,128]{2,1,0:T(8,128)(2,1)S(1)} fusion(f32[128]{0:T(128)} %param.16, f32[16,16]{1,0:T(8,128)S(1)} %dynamic-slice_multiply_fusion, bf16[16,256,128]{2,1,0:T(8,128)(2,1)} %cond_ref.1, s32[]{:T(128)S(6)} %select_n.6), kind=kLoop, calls=%fused_computation | loop fusion | flops 131072 | bytes 132612 | tf_op jit(solution)/shard_map/convert_element_type | solution.py:184
  2.4 0.6 %collective-permute-start = (bf16[16,16,128]{2,1,0:T(8,128)(2,1)S(1)}, bf16[16,16,128]{2,1,0:T(8,128)(2,1)S(1)}, u32[]{:S(2)}, u32[]{:S(2)}) collective-permute-start(bf16[16,16,128]{2,1,0:T(8,128)(2,1)S(1)} %add_convert_fusion), channel_id=1, source_target_pairs={{0,1},{1,0},{2,3},{3,2},{4,5},{5,4},{6,7},{7,6},{8,9},{9,8},{10,11... | collective-permute-start | bytes 196616 | tf_op jit(solution)/shard_map/ppermute | solution.py:188
  3.0 0.9 %collective-permute-done.left_ref.right_ref = bf16[16,16,128]{2,1,0:T(8,128)(2,1)S(1)} collective-permute-done((bf16[16,16,128]{2,1,0:T(8,128)(2,1)S(1)}, bf16[16,16,128]{2,1,0:T(8,128)(2,1)S(1)}, u32[]{:S(2)}, u32[]{:S(2)}) %collective-permute-start) | collective-permute-done | bytes 65568 | tf_op jit(solution)/shard_map/ppermute | solution.py:188
  3.9 0.0 copy-start.2
  3.9 0.6 %copy-done.2 = bf16[16,16,128]{2,1,0:T(8,128)(2,1)} copy-done((bf16[16,16,128]{2,1,0:T(8,128)(2,1)}, bf16[16,16,128]{2,1,0:T(8,128)(2,1)S(1)}, u32[]{:S(2)}) %copy-start.2) | copy-done | bytes 65560
  4.5 3.2 %embed.1.own_ref = bf16[16,2,144,128]{3,2,1,0:T(8,128)(2,1)} custom-call(f32[1]{0:T(128)S(6)} %copy.12.now_ref, bf16[16,256,128]{2,1,0:T(8,128)(2,1)} %cond_ref.1, f32[16,256]{1,0:T(8,128)} %noisy_ref.3, f32[1,128]{1,0:T(1,128)} %bitcast.5, bf16[16,16,128]{2,1,0:T(8,128)(2,1)} %copy-done.2, bf16[16,16,128]{2,1,0:T(8,128)(2,1)} %copy-done.2), custom_call_target="tpu_custom_call" | custom-call | tf_op jit(solution)/shard_map/embed/pallas_call | solution.py:193
  7.8 1.1 %fusion = (bf16[5,2,144,128]{3,2,1,0:T(8,128)(2,1)S(1)}, bf16[5,2,144,128]{3,2,1,0:T(8,128)(2,1)S(1)}) fusion(bf16[16,2,144,128]{3,2,1,0:T(8,128)(2,1)} %embed.1.own_ref), kind=kLoop, calls=%fused_computation.2 | loop fusion | bytes 1474560 | tf_op jit(solution)/shard_map/slice | solution.py:203
  8.9 4.8 %collective-permute-start.1 = (bf16[5,2,144,128]{3,2,1,0:T(8,128)(2,1)S(1)}, bf16[5,2,144,128]{3,2,1,0:T(8,128)(2,1)S(1)}, u32[]{:S(2)}, u32[]{:S(2)}) collective-permute-start(bf16[5,2,144,128]{3,2,1,0:T(8,128)(2,1)S(1)} %get-tuple-element.6), channel_id=1, source_target_pairs={{0,4},{4,8},{8,12},{1,5},{5,9},{9,13},{2,6},{6,10},{10,14},{3,7},{... | collective-permute-start | bytes 1105928 | tf_op jit(solution)/shard_map/ppermute | solution.py:202
  13.8 1.3 %collective-permute-start.2 = (bf16[5,2,144,128]{3,2,1,0:T(8,128)(2,1)S(1)}, bf16[5,2,144,128]{3,2,1,0:T(8,128)(2,1)S(1)}, u32[]{:S(2)}, u32[]{:S(2)}) collective-permute-start(bf16[5,2,144,128]{3,2,1,0:T(8,128)(2,1)S(1)} %get-tuple-element.5), channel_id=1, source_target_pairs={{4,0},{8,4},{12,8},{5,1},{9,5},{13,9},{6,2},{10,6},{14,10},{7,3},{... | collective-permute-start | bytes 1105928 | tf_op jit(solution)/shard_map/ppermute | solution.py:203
  15.7 6.2 %collective-permute-done.1.top_ref = bf16[5,2,144,128]{3,2,1,0:T(8,128)(2,1)S(1)} collective-permute-done((bf16[5,2,144,128]{3,2,1,0:T(8,128)(2,1)S(1)}, bf16[5,2,144,128]{3,2,1,0:T(8,128)(2,1)S(1)}, u32[]{:S(2)}, u32[]{:S(2)}) %collective-permute-start.1) | collective-permute-done | bytes 368672 | tf_op jit(solution)/shard_map/ppermute | solution.py:202
  21.9 0.0 copy-start
  21.9 4.1 %collective-permute-done.2.bot_ref = bf16[5,2,144,128]{3,2,1,0:T(8,128)(2,1)S(1)} collective-permute-done((bf16[5,2,144,128]{3,2,1,0:T(8,128)(2,1)S(1)}, bf16[5,2,144,128]{3,2,1,0:T(8,128)(2,1)S(1)}, u32[]{:S(2)}, u32[]{:S(2)}) %collective-permute-start.2) | collective-permute-done | bytes 368672 | tf_op jit(solution)/shard_map/ppermute | solution.py:203
  26.0 0.0 copy-start.1
  26.0 0.0 copy-done
  26.0 0.7 %copy-done.1 = bf16[5,2,144,128]{3,2,1,0:T(8,128)(2,1)} copy-done((bf16[5,2,144,128]{3,2,1,0:T(8,128)(2,1)}, bf16[5,2,144,128]{3,2,1,0:T(8,128)(2,1)S(1)}, u32[]{:S(2)}) %copy-start.1) | copy-done | bytes 368664
  26.8 11.3 %step.1 = f32[16,256]{1,0:T(8,128)} custom-call(f32[1]{0:T(128)S(6)} %copy.12.now_ref, f32[1]{0:T(128)S(6)} %copy.13.next_ref, bf16[16,2,144,128]{3,2,1,0:T(8,128)(2,1)} %embed.1.own_ref, bf16[5,2,144,128]{3,2,1,0:T(8,128)(2,1)} %copy-done, bf16[5,2,144,128]{3,2,1,0:T(8,128)(2,1)} %copy-done.1, bf16[2,9,128,128]{3,2,1,0:T(8,128)(2,1)} %fine_ref.1, ...), custom_call_target="tpu_custom_call" | custom-call | tf_op jit(solution)/shard_map/step/pallas_call | solution.py:205
Async XLA Ops:
  2.4 1.5 %collective-permute-start = (bf16[16,16,128]{2,1,0:T(8,128)(2,1)S(1)}, bf16[16,16,128]{2,1,0:T(8,128)(2,1)S(1)}, u32[]{:S(2)}, u32[]{:S(2)}) collective-permute-start(bf16[16,16,128]{2,1,0:T(8,128)(2,1)S(1)} %add_convert_fusion), channel_id=1, source_target_pairs={{0,1},{1,0},{2,3},{3,2},{4,5},{5,4},{6,7},{7,6},{8,9},{9,8},{10,11... | collective-permute-start | bytes 196616 | tf_op jit(solution)/shard_map/ppermute | solution.py:188
  3.9 0.6 %copy-start.2 = (bf16[16,16,128]{2,1,0:T(8,128)(2,1)}, bf16[16,16,128]{2,1,0:T(8,128)(2,1)S(1)}, u32[]{:S(2)}) copy-start(bf16[16,16,128]{2,1,0:T(8,128)(2,1)S(1)} %collective-permute-done.left_ref.right_ref) | copy-start | bytes 196612
  8.9 13.0 %collective-permute-start.1 = (bf16[5,2,144,128]{3,2,1,0:T(8,128)(2,1)S(1)}, bf16[5,2,144,128]{3,2,1,0:T(8,128)(2,1)S(1)}, u32[]{:S(2)}, u32[]{:S(2)}) collective-permute-start(bf16[5,2,144,128]{3,2,1,0:T(8,128)(2,1)S(1)} %get-tuple-element.6), channel_id=1, source_target_pairs={{0,4},{4,8},{8,12},{1,5},{5,9},{9,13},{2,6},{6,10},{10,14},{3,7},{... | collective-permute-start | bytes 1105928 | tf_op jit(solution)/shard_map/ppermute | solution.py:202
  13.8 12.3 %collective-permute-start.2 = (bf16[5,2,144,128]{3,2,1,0:T(8,128)(2,1)S(1)}, bf16[5,2,144,128]{3,2,1,0:T(8,128)(2,1)S(1)}, u32[]{:S(2)}, u32[]{:S(2)}) collective-permute-start(bf16[5,2,144,128]{3,2,1,0:T(8,128)(2,1)S(1)} %get-tuple-element.5), channel_id=1, source_target_pairs={{4,0},{8,4},{12,8},{5,1},{9,5},{13,9},{6,2},{10,6},{14,10},{7,3},{... | collective-permute-start | bytes 1105928 | tf_op jit(solution)/shard_map/ppermute | solution.py:203
  21.9 4.1 %copy-start = (bf16[5,2,144,128]{3,2,1,0:T(8,128)(2,1)}, bf16[5,2,144,128]{3,2,1,0:T(8,128)(2,1)S(1)}, u32[]{:S(2)}) copy-start(bf16[5,2,144,128]{3,2,1,0:T(8,128)(2,1)S(1)} %collective-permute-done.1.top_ref) | copy-start | bytes 1105924
  26.0 0.7 %copy-start.1 = (bf16[5,2,144,128]{3,2,1,0:T(8,128)(2,1)}, bf16[5,2,144,128]{3,2,1,0:T(8,128)(2,1)S(1)}, u32[]{:S(2)}) copy-start(bf16[5,2,144,128]{3,2,1,0:T(8,128)(2,1)S(1)} %collective-permute-done.2.bot_ref) | copy-start | bytes 1105924

commit v2 on v1

--- a/solution.py
+++ b/solution.py
@@ -27,7 +27,7 @@
     return inside.astype(F32)
 
 
-def embed_kernel(now_ref, cond_ref, noisy_ref, proj_ref, left_ref, right_ref, out_ref, wide, edge, *, sub, count):
+def embed_kernel(now_ref, cond_ref, noisy_ref, proj_ref, left_ref, right_ref, out_ref, up_ref, dn_ref, wide, edge, *, sub, count):
     rows, cols, _ = cond_ref.shape
     index = lax.axis_index(sub)
     level = jnp.full((1, 128), now_ref[0], F32)
@@ -45,7 +45,12 @@
             main = wide[r % 2, pl.ds(q, cols // 2, stride=2), :]
             lt = edge[r % 2, pl.ds(q, PER, stride=2), :]
             rt = edge[r % 2, pl.ds(EDGE + q, PER, stride=2), :]
-            out_ref[r, q] = jnp.concatenate([main, rt, lt], axis=0).astype(BF16)
+            full = jnp.concatenate([main, rt, lt], axis=0).astype(BF16)
+            out_ref[r, q] = full
+            if r < HALO:
+                dn_ref[r, q] = full
+            if r >= rows - HALO:
+                up_ref[r - rows + HALO, q] = full
 
 
 def step_kernel(
@@ -160,6 +165,10 @@
     noisy = noisy_ref[...]
     denoised = scale_skip * noisy + scale_out * network
     out_ref[...] = denoised + ratio * (noisy - denoised) + spread_by * noise_ref[...]
+
+
+def near(*arrays):
+    return [pltpu.with_memory_space_constraint(a, pltpu.VMEM) for a in arrays]
 
 
 def per_device(
@@ -190,17 +199,18 @@
         left = lax.ppermute(edge_at(cols - EDGE), "sub", [(i, i + 1) for i in range(subs - 1)])
         right = lax.ppermute(edge_at(0), "sub", [(i + 1, i) for i in range(subs - 1)])
 
-    mine = pl.pallas_call(
+    mine, upward, downward = pl.pallas_call(
         functools.partial(embed_kernel, sub="sub", count=subs),
-        out_shape=jax.ShapeDtypeStruct((rows, 2, ring, c1), BF16),
+        out_shape=[pltpu.VMEM((n, 2, ring, c1), BF16) for n in (rows, HALO, HALO)],
         in_specs=[smem] + [vmem] * 5,
-        out_specs=vmem,
+        out_specs=[vmem] * 3,
         scratch_shapes=[pltpu.VMEM((2, cols, c1), F32), pltpu.VMEM((2, 2 * EDGE, c1), F32)],
+        compiler_params=pltpu.CompilerParams(vmem_limit_bytes=24 << 20),
         name="embed",
-    )(sigma_now, cond_features, noisy_field, field_proj[None], left, right)
-
-    top = lax.ppermute(mine[rows - HALO :], "patch", [(i, i + 1) for i in range(patches - 1)])
-    bot = lax.ppermute(mine[:HALO], "patch", [(i + 1, i) for i in range(patches - 1)])
+    )(sigma_now, cond_features, noisy_field, field_proj[None], *near(left, right))
+
+    top = lax.ppermute(upward, "patch", [(i, i + 1) for i in range(patches - 1)])
+    bot = lax.ppermute(downward, "patch", [(i + 1, i) for i in range(patches - 1)])
 
     return pl.pallas_call(
         functools.partial(step_kernel, patch="patch", patches=patches, sub="sub", subs=subs),
@@ -218,10 +228,12 @@
             pltpu.VMEM((2, rows, own, c1), BF16),
             pltpu.VMEM((cols, 128), F32),
         ],
+        compiler_params=pltpu.CompilerParams(vmem_limit_bytes=32 << 20),
         name="step",
     )(
-        sigma_now, sigma_next, mine, top, bot, fine_kernels, coarse_kernel.reshape(9 * c2, c2),
-        down_proj, up_proj, out_proj[None], noisy_field, noise_draw,
+        sigma_now, sigma_next,
+        *near(mine, top, bot, fine_kernels, coarse_kernel.reshape(9 * c2, c2), down_proj, up_proj),
+        out_proj[None], noisy_field, noise_draw,
     )
 
 

time: 38.3 us -> 35.4 us (0.924)
  Pallas kernels: 14.5 us -> 10.2 us
  local copies, waits for them, and re-layouts: 2.5 us -> 3.68 us
    unnamed x6 -> x20, local copies, waits for them, and re-layouts: 1.36 us -> 3.68 us
    pallas_call x1, Pallas kernels: 3.24 us -> 0.94 us  [per_device(): pl.pallas_call(functools.partial(embed_kernel, sub='sub', count=subs), ou...]
    pallas_call x1, Pallas kernels: 11.3 us -> 9.23 us  [per_device(): pl.pallas_call(functools.partial(step_kernel, patch='patch', patches=patc...]
    slice x1 -> x0, local copies, waits for them, and re-layouts: 1.15 us -> none  [per_device(): mine[:HALO]]
where the time goes in v2:
time: 35.4 us; the launch traced here: 35 us
  waiting for transfers between devices  11.2 us (32%)
  Pallas kernels  10.2 us (29%)
  starting transfers between devices  6.71 us (19%)
  local copies, waits for them, and re-layouts  3.68 us (10%)
  other arithmetic  1.73 us (5%)
  between operations  1.46 us (4%)
    pallas_call x1, Pallas kernels, per_device(): pl.pallas_call(functools.partial(step_kernel, patch='patch', patches=patc...  9.23 us
    ppermute x1, waiting for transfers between devices, per_device(): lax.ppermute(upward, 'patch', [(i, i + 1) for i in range(patches - 1)])  6.18 us
    ppermute x1, starting transfers between devices, per_device(): lax.ppermute(upward, 'patch', [(i, i + 1) for i in range(patches - 1)])  4.84 us
    ppermute x1, waiting for transfers between devices, per_device(): lax.ppermute(downward, 'patch', [(i + 1, i) for i in range(patches - 1)])  4.14 us
    unnamed x20, local copies, waits for them, and re-layouts  3.68 us
    ppermute x1, starting transfers between devices, per_device(): lax.ppermute(downward, 'patch', [(i + 1, i) for i in range(patches - 1)])  1.29 us
    convert_element_type x1, other arithmetic, edge_at(): (cond.astype(F32) + (scale_in * noisy)[:, :, None] * field_proj).astype(B...  0.96 us
    pallas_call x1, Pallas kernels, per_device(): pl.pallas_call(functools.partial(embed_kernel, sub='sub', count=subs), ou...  0.94 us
  transfers between devices with their start and end apart: 3, of which 3 were waited for; matrix products, arithmetic and copies ran while one was open for 0% of the time, Pallas kernels for 0%

profile of v2, /device:TPU:0, one launch (start us, length us, event | category | flops | bytes accessed | tf_op | source)
XLA Modules:
  0.0 35.0 jit_solution(10704767759855119111)
XLA Ops:
  0.0 0.0 copy-start.4
  0.0 0.0 copy-start.9
  0.0 0.0 copy-start.7
  0.0 0.0 copy-start.5
  0.0 0.0 copy-start.6
  0.8 0.8 %dynamic-slice_multiply_fusion = f32[16,16]{1,0:T(8,128)S(1)} fusion(f32[16,256]{1,0:T(8,128)} %noisy_ref.3, s32[]{:T(128)S(6)} %select_n.6, f32[]{:T(128)} %bitcast.1), kind=kLoop, calls=%fused_computation.1 | loop fusion | flops 256 | bytes 2056 | tf_op jit(solution)/shard_map/mul | solution.py:193
  1.5 1.0 %add_convert_fusion = bf16[16,16,128]{2,1,0:T(8,128)(2,1)S(1)} fusion(f32[128]{0:T(128)} %param.16, f32[16,16]{1,0:T(8,128)S(1)} %dynamic-slice_multiply_fusion, bf16[16,256,128]{2,1,0:T(8,128)(2,1)} %cond_ref.1, s32[]{:T(128)S(6)} %select_n.6), kind=kLoop, calls=%fused_computation | loop fusion | flops 131072 | bytes 132612 | tf_op jit(solution)/shard_map/convert_element_type | solution.py:193
  2.5 0.6 %collective-permute-start = (bf16[16,16,128]{2,1,0:T(8,128)(2,1)S(1)}, bf16[16,16,128]{2,1,0:T(8,128)(2,1)S(1)}, u32[]{:S(2)}, u32[]{:S(2)}) collective-permute-start(bf16[16,16,128]{2,1,0:T(8,128)(2,1)S(1)} %add_convert_fusion), channel_id=1, source_target_pairs={{0,1},{1,0},{2,3},{3,2},{4,5},{5,4},{6,7},{7,6},{8,9},{9,8},{10,11... | collective-permute-start | bytes 196616 | tf_op jit(solution)/shard_map/ppermute | solution.py:197
  3.1 0.9 %collective-permute-done.left_ref.right_ref = bf16[16,16,128]{2,1,0:T(8,128)(2,1)S(1)} collective-permute-done((bf16[16,16,128]{2,1,0:T(8,128)(2,1)S(1)}, bf16[16,16,128]{2,1,0:T(8,128)(2,1)S(1)}, u32[]{:S(2)}, u32[]{:S(2)}) %collective-permute-start) | collective-permute-done | bytes 65568 | tf_op jit(solution)/shard_map/ppermute | solution.py:197
  4.0 0.0 copy-start
  4.0 1.2 %copy-done = bf16[16,256,128]{2,1,0:T(8,128)(2,1)S(1)} copy-done((bf16[16,256,128]{2,1,0:T(8,128)(2,1)S(1)}, bf16[16,256,128]{2,1,0:T(8,128)(2,1)}, u32[]{:S(2)}) %copy-start) | copy-done | bytes 1048600
  5.2 0.0 copy-start.3
  5.2 0.7 %copy-done.3 = f32[16,256]{1,0:T(8,128)S(1)} copy-done((f32[16,256]{1,0:T(8,128)S(1)}, f32[16,256]{1,0:T(8,128)}, u32[]{:S(2)}) %copy-start.3) | copy-done | bytes 16408
  5.9 0.0 copy-start.8
  5.9 0.7 %copy-done.8 = f32[128]{0:T(128)S(1)} copy-done((f32[128]{0:T(128)S(1)}, f32[128]{0:T(128)}, u32[]{:S(2)}) %copy-start.8) | copy-done | bytes 536
  6.6 0.0 copy-start.1
  6.6 0.9 %embed.1 = (bf16[16,2,144,128]{3,2,1,0:T(8,128)(2,1)S(1)}, bf16[5,2,144,128]{3,2,1,0:T(8,128)(2,1)S(1)}, bf16[5,2,144,128]{3,2,1,0:T(8,128)(2,1)S(1)}) custom-call(f32[1]{0:T(128)S(6)} %copy.12.now_ref, bf16[16,256,128]{2,1,0:T(8,128)(2,1)S(1)} %copy-done, f32[16,256]{1,0:T(8,128)S(1)} %copy-done.3, f32[1,128]{1,0:T(1,128)S(1)} %bitcast.5, ...), custom_call_target="tpu_custom_call" | custom-call | tf_op jit(solution)/shard_map/embed/pallas_call | solution.py:202
  7.5 4.8 %collective-permute-start.1 = (bf16[5,2,144,128]{3,2,1,0:T(8,128)(2,1)S(1)}, bf16[5,2,144,128]{3,2,1,0:T(8,128)(2,1)S(1)}, u32[]{:S(2)}, u32[]{:S(2)}) collective-permute-start(bf16[5,2,144,128]{3,2,1,0:T(8,128)(2,1)S(1)} %get-tuple-element.9), channel_id=1, source_target_pairs={{0,4},{4,8},{8,12},{1,5},{5,9},{9,13},{2,6},{6,10},{10,14},{3,7},{... | collective-permute-start | bytes 1105928 | tf_op jit(solution)/shard_map/ppermute | solution.py:212
  12.4 1.3 %collective-permute-start.2 = (bf16[5,2,144,128]{3,2,1,0:T(8,128)(2,1)S(1)}, bf16[5,2,144,128]{3,2,1,0:T(8,128)(2,1)S(1)}, u32[]{:S(2)}, u32[]{:S(2)}) collective-permute-start(bf16[5,2,144,128]{3,2,1,0:T(8,128)(2,1)S(1)} %get-tuple-element.10), channel_id=1, source_target_pairs={{4,0},{8,4},{12,8},{5,1},{9,5},{13,9},{6,2},{10,6},{14,10},{7,3},{... | collective-permute-start | bytes 1105928 | tf_op jit(solution)/shard_map/ppermute | solution.py:213
  14.3 6.2 %collective-permute-done.1.top_ref = bf16[5,2,144,128]{3,2,1,0:T(8,128)(2,1)S(1)} collective-permute-done((bf16[5,2,144,128]{3,2,1,0:T(8,128)(2,1)S(1)}, bf16[5,2,144,128]{3,2,1,0:T(8,128)(2,1)S(1)}, u32[]{:S(2)}, u32[]{:S(2)}) %collective-permute-start.1) | collective-permute-done | bytes 368672 | tf_op jit(solution)/shard_map/ppermute | solution.py:212
  20.5 4.1 %collective-permute-done.2.bot_ref = bf16[5,2,144,128]{3,2,1,0:T(8,128)(2,1)S(1)} collective-permute-done((bf16[5,2,144,128]{3,2,1,0:T(8,128)(2,1)S(1)}, bf16[5,2,144,128]{3,2,1,0:T(8,128)(2,1)S(1)}, u32[]{:S(2)}, u32[]{:S(2)}) %collective-permute-start.2) | collective-permute-done | bytes 368672 | tf_op jit(solution)/shard_map/ppermute | solution.py:213
  24.6 0.0 copy-done.4
  24.6 0.0 copy-done.9
  24.6 0.0 copy-done.7
  24.6 0.0 copy-done.5
  24.7 0.0 copy-done.6
  24.7 0.0 copy-done.1
  24.7 0.0 copy-start.2
  24.7 1.1 %copy-done.2 = bf16[2,9,128,128]{3,2,1,0:T(8,128)(2,1)S(1)} copy-done((bf16[2,9,128,128]{3,2,1,0:T(8,128)(2,1)S(1)}, bf16[2,9,128,128]{3,2,1,0:T(8,128)(2,1)}, u32[]{:S(2)}) %copy-start.2) | copy-done | bytes 589848
  25.7 9.2 %step.1 = f32[16,256]{1,0:T(8,128)} custom-call(f32[1]{0:T(128)S(6)} %copy.12.now_ref, f32[1]{0:T(128)S(6)} %copy.13.next_ref, bf16[16,2,144,128]{3,2,1,0:T(8,128)(2,1)S(1)} %get-tuple-element.8.own_ref, bf16[5,2,144,128]{3,2,1,0:T(8,128)(2,1)S(1)} %collective-permute-done.1.top_ref, bf16[5,2,144,128]{3,2,1,0:T(8,128)(2,1)S(1)} %collective-permute-done.2.bot_ref, ...), custom_call_target="tpu_custom_call" | custom-call | tf_op jit(solution)/shard_map/step/pallas_call | solution.py:215
Async XLA Ops:
  0.0 24.6 %copy-start.4 = (f32[16,256]{1,0:T(8,128)S(1)}, f32[16,256]{1,0:T(8,128)}, u32[]{:S(2)}) copy-start(f32[16,256]{1,0:T(8,128)} %noisy_ref.3) | copy-start | bytes 49156
  0.0 24.6 %copy-start.9 = (bf16[128]{0:T(256)(128)(2,1)S(1)}, bf16[128]{0:T(256)(128)(2,1)}, u32[]{:S(2)}) copy-start(bf16[128]{0:T(256)(128)(2,1)} %param.21) | copy-start | bytes 772
  0.0 24.6 %copy-start.7 = (f32[16,256]{1,0:T(8,128)S(1)}, f32[16,256]{1,0:T(8,128)}, u32[]{:S(2)}) copy-start(f32[16,256]{1,0:T(8,128)} %noise_ref.1) | copy-start | bytes 49156
  0.0 24.6 %copy-start.5 = (bf16[128,256]{1,0:T(8,128)(2,1)S(1)}, bf16[128,256]{1,0:T(8,128)(2,1)}, u32[]{:S(2)}) copy-start(bf16[128,256]{1,0:T(8,128)(2,1)} %down_ref.1) | copy-start | bytes 196612
  0.0 24.6 %copy-start.6 = (bf16[256,128]{1,0:T(8,128)(2,1)S(1)}, bf16[256,128]{1,0:T(8,128)(2,1)}, u32[]{:S(2)}) copy-start(bf16[256,128]{1,0:T(8,128)(2,1)} %up_ref.1) | copy-start | bytes 196612
  2.5 1.5 %collective-permute-start = (bf16[16,16,128]{2,1,0:T(8,128)(2,1)S(1)}, bf16[16,16,128]{2,1,0:T(8,128)(2,1)S(1)}, u32[]{:S(2)}, u32[]{:S(2)}) collective-permute-start(bf16[16,16,128]{2,1,0:T(8,128)(2,1)S(1)} %add_convert_fusion), channel_id=1, source_target_pairs={{0,1},{1,0},{2,3},{3,2},{4,5},{5,4},{6,7},{7,6},{8,9},{9,8},{10,11... | collective-permute-start | bytes 196616 | tf_op jit(solution)/shard_map/ppermute | solution.py:197
  4.0 1.2 %copy-start = (bf16[16,256,128]{2,1,0:T(8,128)(2,1)S(1)}, bf16[16,256,128]{2,1,0:T(8,128)(2,1)}, u32[]{:S(2)}) copy-start(bf16[16,256,128]{2,1,0:T(8,128)(2,1)} %cond_ref.1) | copy-start | bytes 3145732
  5.2 0.7 %copy-start.3 = (f32[16,256]{1,0:T(8,128)S(1)}, f32[16,256]{1,0:T(8,128)}, u32[]{:S(2)}) copy-start(f32[16,256]{1,0:T(8,128)} %noisy_ref.3) | copy-start | bytes 49156
  5.9 0.7 %copy-start.8 = (f32[128]{0:T(128)S(1)}, f32[128]{0:T(128)}, u32[]{:S(2)}) copy-start(f32[128]{0:T(128)} %param.16) | copy-start | bytes 1540
  6.6 18.1 %copy-start.1 = (bf16[9,256,256]{2,1,0:T(8,128)(2,1)S(1)}, bf16[9,256,256]{2,1,0:T(8,128)(2,1)}, u32[]{:S(2)}) copy-start(bf16[9,256,256]{2,1,0:T(8,128)(2,1)} %param.18) | copy-start | bytes 3538948
  7.5 13.0 %collective-permute-start.1 = (bf16[5,2,144,128]{3,2,1,0:T(8,128)(2,1)S(1)}, bf16[5,2,144,128]{3,2,1,0:T(8,128)(2,1)S(1)}, u32[]{:S(2)}, u32[]{:S(2)}) collective-permute-start(bf16[5,2,144,128]{3,2,1,0:T(8,128)(2,1)S(1)} %get-tuple-element.9), channel_id=1, source_target_pairs={{0,4},{4,8},{8,12},{1,5},{5,9},{9,13},{2,6},{6,10},{10,14},{3,7},{... | collective-permute-start | bytes 1105928 | tf_op jit(solution)/shard_map/ppermute | solution.py:212
  12.4 12.3 %collective-permute-start.2 = (bf16[5,2,144,128]{3,2,1,0:T(8,128)(2,1)S(1)}, bf16[5,2,144,128]{3,2,1,0:T(8,128)(2,1)S(1)}, u32[]{:S(2)}, u32[]{:S(2)}) collective-permute-start(bf16[5,2,144,128]{3,2,1,0:T(8,128)(2,1)S(1)} %get-tuple-element.10), channel_id=1, source_target_pairs={{4,0},{8,4},{12,8},{5,1},{9,5},{13,9},{6,2},{10,6},{14,10},{7,3},{... | collective-permute-start | bytes 1105928 | tf_op jit(solution)/shard_map/ppermute | solution.py:213
  24.7 1.1 %copy-start.2 = (bf16[2,9,128,128]{3,2,1,0:T(8,128)(2,1)S(1)}, bf16[2,9,128,128]{3,2,1,0:T(8,128)(2,1)}, u32[]{:S(2)}) copy-start(bf16[2,9,128,128]{3,2,1,0:T(8,128)(2,1)} %fine_ref.1) | copy-start | bytes 1769476

commit v3 on v0

v3 whole, which is shorter than its diff:
```python
import functools

import jax
import jax.numpy as jnp
from jax import lax
from jax.experimental import pallas as pl
from jax.experimental.pallas import tpu as pltpu
from jax.sharding import PartitionSpec as P

F32 = jnp.float32
BF16 = jnp.bfloat16
HALO = 5
EDGE = 16
PER = EDGE // 2
CHUNK = 3


def silu(v):
    half = 0.5 * v
    return half + half * jnp.tanh(half)


def flag(condition):
    return jnp.where(condition, 1.0, 0.0).astype(F32)


class Place:
    def __init__(self, sizes, pieces):
        self.piece = lax.rem(lax.axis_index("fsdp"), pieces)
        self.sub = lax.axis_index("sub")
        self.patch = lax.axis_index("patch")
        self.first = self.piece == 0
        self.last = self.piece == pieces - 1
        self.has_left = jnp.logical_or(self.piece > 0, self.sub > 0)
        self.has_right = jnp.logical_or(self.piece < pieces - 1, self.sub < sizes["sub"] - 1)
        self.above = flag(self.patch > 0)
        self.below = flag(self.patch < sizes["patch"] - 1)

    def column_mask(self, ring, own):
        at = lax.broadcasted_iota(jnp.int32, (ring, 128), 0)
        return jnp.where(at < own, 1.0, jnp.where(at < own + PER, flag(self.has_right), flag(self.has_left)))


def embed_kernel(
    now_ref, cond_ref, noisy_ref, proj_ref, mine_ref, tile_ref, send_ref,
    main, inner, give, field, embedding, turned, wide, edge, sems, *, sizes, pieces,
):
    rows, window, _ = main.shape
    cols = noisy_ref.shape[1]
    place = Place(sizes, pieces)
    start = pl.multiple_of(place.piece * window, EDGE)
    near_by = pl.multiple_of(jnp.where(place.first, window, start - EDGE), EDGE)
    given = pl.multiple_of(jnp.where(place.sub == 0, cols - EDGE, 0), EDGE)
    small = [
        pltpu.make_async_copy(noisy_ref, field, sems.at[3]),
        pltpu.make_async_copy(proj_ref, embedding, sems.at[4]),
    ]
    copies = [pltpu.make_async_copy(cond_ref.at[:, pl.ds(given, EDGE)], give, sems.at[0])]
    if pieces > 1:
        copies.append(pltpu.make_async_copy(cond_ref.at[:, pl.ds(near_by, EDGE)], inner, sems.at[1]))
    copies.append(pltpu.make_async_copy(cond_ref.at[:, pl.ds(start, window)], main, sems.at[2]))
    for copy in small + copies:
        copy.start()
    level = jnp.full((1, 128), now_ref[0], F32)
    scale_in = 1.0 / jnp.sqrt(level * level + 1.0)
    for copy in small:
        copy.wait()
    turned[:, :rows] = jnp.transpose(field[...] * scale_in[:, :1])
    proj = embedding[...]

    def hidden(buf, r, at):
        return buf[r].astype(F32) + turned[pl.ds(at, buf.shape[1]), r : r + 1] * proj

    for copy in copies[:-1]:
        copy.wait()
    for r in range(rows):
        edge[r % 2, :EDGE] = hidden(give, r, given)
        for q in range(2):
            send_ref[r, q] = edge[r % 2, pl.ds(q, PER, stride=2), :].astype(BF16)
        if pieces > 1:
            edge[r % 2, EDGE:] = hidden(inner, r, near_by)
            for q in range(2):
                block = edge[r % 2, pl.ds(EDGE + q, PER, stride=2), :]
                to_right = block * flag(jnp.logical_not(place.last))
                to_left = block * flag(jnp.logical_not(place.first))
                tile_ref[r, q] = jnp.concatenate([to_right, to_left], axis=0).astype(BF16)
        else:
            tile_ref[r] = jnp.zeros_like(tile_ref[r])
    copies[-1].wait()
    for r in range(rows):
        wide[r % 2] = hidden(main, r, start)
        for q in range(2):
            mine_ref[r, q] = wide[r % 2, pl.ds(q, window // 2, stride=2), :].astype(BF16)


def border_kernel(mine_ref, tile_ref, got_ref, full_ref, up_ref, down_ref, *, sizes, pieces):
    rows, _, own, _ = mine_ref.shape
    place = Place(sizes, pieces)
    right = flag(jnp.logical_and(place.last, place.has_right))
    left = flag(jnp.logical_and(place.first, place.has_left))
    for r in range(rows):
        for q in range(2):
            got = got_ref[r, q].astype(F32)
            tile = tile_ref[r, q].astype(F32) + jnp.concatenate([got * right, got * left], axis=0)
            tile = tile.astype(BF16)
            full_ref[r, q] = tile
            for ref, at in ((down_ref, r), (up_ref, r - rows + HALO)):
                if 0 <= at < HALO:
                    ref[at, q, :own] = mine_ref[r, q]
                    ref[at, q, own:] = tile


def put_planes(ref, at, even, odd):
    ring = even.shape[0]
    ref[at, 0] = even.astype(BF16)
    ref[at, 1] = odd.astype(BF16)
    ref[at, 2] = pltpu.roll(odd, 1, 0).astype(BF16)
    ref[at, 3] = pltpu.roll(even, ring - 1, 0).astype(BF16)


def chunks(rows_of):
    return [rows_of[k : k + CHUNK] for k in range(0, len(rows_of), CHUNK)]


def conv_pairs(planes_of, pairs, weight):
    parts = []
    for i in pairs:
        found = [planes_of(2 * i - 1 + d) for d in range(4)]
        for planes in ((2, 0, 1), (0, 1, 3)):
            parts.append(jnp.concatenate([ref[at, k] for k in planes for ref, at in found], axis=1))
    return jnp.dot(jnp.concatenate(parts, axis=0), weight[...], preferred_element_type=F32)


def first_conv(planes_of, h1_of, pool_ref, slot_of, pairs, weight, ring, c1):
    for group in chunks(pairs):
        acc = conv_pairs(planes_of, group, weight)
        for n, i in enumerate(group):
            total = None
            for o in range(2):
                ref, at = planes_of(2 * i + o)
                for q in range(2):
                    v = acc[(2 * n + q) * ring : (2 * n + q + 1) * ring, o * c1 : (o + 1) * c1]
                    h = (ref[at, q].astype(F32) + silu(v)).astype(BF16)
                    kept = h1_of(2 * i + o)
                    if kept is not None:
                        kept[0][kept[1], q] = h
                    total = h.astype(F32) if total is None else total + h.astype(F32)
            pool_ref[slot_of(i) * ring : (slot_of(i) + 1) * ring] = (total * 0.25).astype(BF16)


def coarse_in(pool_ref, down_ref, ci_of, order, mask_of, ring, c2):
    ci_all = jnp.dot(pool_ref[...], down_ref[...], preferred_element_type=F32)
    for n, i in enumerate(order):
        ci = ci_all[n * ring : (n + 1) * ring] * jnp.concatenate([mask_of(i)] * (c2 // 128), axis=1)
        ref, at = ci_of(i)
        ref[at, 0] = pltpu.roll(ci, 1, 0).astype(BF16)
        ref[at, 1] = ci.astype(BF16)
        ref[at, 2] = pltpu.roll(ci, ring - 1, 0).astype(BF16)


def coarse_conv(ci_of, co_ref, order, coarse_ref, ring):
    for k, group in enumerate(chunks(order)):
        parts = []
        for i in group:
            found = [ci_of(i - 1 + a) for a in range(3)]
            parts.append(jnp.concatenate([ref[at, b] for ref, at in found for b in range(3)], axis=1))
        v = jnp.dot(jnp.concatenate(parts, axis=0), coarse_ref[...], preferred_element_type=F32)
        for n, i in enumerate(group):
            ref, at = ci_of(i)
            slot = k * CHUNK + n
            co = ref[at, 1].astype(F32) + silu(v[n * ring : (n + 1) * ring])
            co_ref[slot * ring : (slot + 1) * ring] = co.astype(BF16)


def lift(co_ref, up_ref, order, h1_of, h2_of, mask_of, wanted, ring):
    lifted_all = jnp.dot(co_ref[...], up_ref[...], preferred_element_type=F32)
    for n, i in enumerate(order):
        lifted = lifted_all[n * ring : (n + 1) * ring]
        for r in (2 * i, 2 * i + 1):
            if r in wanted:
                ref, at = h1_of(r)
                mask = mask_of(r)
                into, slot = h2_of(r)
                put_planes(into, slot, (ref[at, 0].astype(F32) + lifted) * mask, (ref[at, 1].astype(F32) + lifted) * mask)


def second_conv(h2_of, h3_of, pairs, weight, ring, own, c1):
    for group in chunks(pairs):
        acc = conv_pairs(h2_of, group, weight)
        for n, i in enumerate(group):
            for o in range(2):
                ref, at = h2_of(2 * i + o)
                into, slot = h3_of(2 * i + o)
                for q in range(2):
                    v = acc[(2 * n + q) * ring : (2 * n + q) * ring + own, o * c1 : (o + 1) * c1]
                    into[q, slot] = (ref[at, q, :own].astype(F32) + silu(v)).astype(BF16)


def inner_kernel(
    mine_ref, tile_ref, fine_ref, coarse_ref, down_ref, up_ref,
    x_ref, w_ref, h1_ref, ci_ref, h2_ref, h3_ref, pool_ref, co_ref, *, sizes, pieces,
):
    rows, _, own, c1 = mine_ref.shape
    ring = own + EDGE
    c2 = down_ref.shape[1]
    half = rows // 2
    mask = Place(sizes, pieces).column_mask(ring, own)
    for layer in range(2):
        for b in range(3):
            for d in range(4):
                at = (b * 4 + d) * c1
                for o in range(2):
                    a = d - o
                    block = fine_ref[layer, a * 3 + b] if 0 <= a <= 2 else jnp.zeros((c1, c1), BF16)
                    w_ref[layer, at : at + c1, o * c1 : (o + 1) * c1] = block
    for r in range(rows):
        even, odd = (jnp.concatenate([mine_ref[r, q].astype(F32), tile_ref[r, q].astype(F32)], axis=0) for q in range(2))
        put_planes(x_ref, r, even, odd)
    x_of = lambda r: (x_ref, r)
    h1_of = lambda r: (h1_ref, r - 2)
    ci_of = lambda i: (ci_ref, i - 1)
    h2_of = lambda r: (h2_ref, r - 4)
    h3_of = lambda r: (h3_ref, r - 6)
    first_conv(x_of, h1_of, pool_ref, lambda i: i - 1, list(range(1, half - 1)), w_ref.at[0], ring, c1)
    coarse_in(pool_ref, down_ref, ci_of, range(1, half - 1), lambda i: mask, ring, c2)
    coarse_conv(ci_of, co_ref, list(range(2, half - 2)), coarse_ref, ring)
    lift(co_ref, up_ref, range(2, half - 2), h1_of, h2_of, lambda r: mask, range(4, rows - 4), ring)
    second_conv(h2_of, h3_of, list(range(3, half - 3)), w_ref.at[1], ring, own, c1)


def outer_kernel(
    now_ref, next_ref, top_ref, bot_ref, xin_ref, w_ref, h1in_ref, ciin_ref, h2in_ref, h3in_ref,
    coarse_ref, down_ref, up_ref, outp_ref, noisy_ref, noise_ref, out_ref,
    x_ref, pool_ref, h1_ref, ci_ref, co_ref, h2_ref, h3_ref, flat_ref, *, sizes, pieces,
):
    rows, _, ring, c1 = xin_ref.shape
    own = ring - EDGE
    c2 = down_ref.shape[1]
    half = rows // 2
    place = Place(sizes, pieces)
    inside = place.column_mask(ring, own)

    def mask_to(extent):
        return lambda r: inside * place.above if r < 0 else inside * place.below if r >= extent else inside

    for n in range(HALO):
        put_planes(x_ref, n, top_ref[n, 0].astype(F32), top_ref[n, 1].astype(F32))
        put_planes(x_ref, HALO + n, bot_ref[n, 0].astype(F32), bot_ref[n, 1].astype(F32))

    def x_of(r):
        return (x_ref, r + HALO) if r < 0 else (xin_ref, r) if r < rows else (x_ref, HALO + r - rows)

    def h1_of(r):
        if 2 <= r < rows - 2:
            return h1in_ref, r - 2
        if -1 <= r < 2:
            return h1_ref, r + 1
        return (h1_ref, 3 + r - (rows - 2)) if rows - 2 <= r <= rows else None

    def ci_of(i):
        if 1 <= i < half - 1:
            return ciin_ref, i - 1
        return (ci_ref, i + 2) if i < 1 else (ci_ref, 3 + i - (half - 1))

    def h2_of(r):
        if 4 <= r < rows - 4:
            return h2in_ref, r - 4
        return (h2_ref, r + 1) if r < 4 else (h2_ref, 5 + r - (rows - 4))

    def h3_of(r):
        return (h3in_ref, r - 6) if 6 <= r < rows - 6 else (h3_ref, r) if r < 6 else (h3_ref, 6 + r - (rows - 6))

    pairs = [-2, -1, 0, half - 1, half, half + 1]
    first_conv(x_of, h1_of, pool_ref, pairs.index, pairs, w_ref.at[0], ring, c1)
    coarse_in(pool_ref, down_ref, ci_of, pairs, mask_to(half), ring, c2)
    order = [-1, 0, 1, half - 2, half - 1, half]
    coarse_conv(ci_of, co_ref, order, coarse_ref, ring)
    wanted = [r for r in range(-1, rows + 1) if not 4 <= r < rows - 4]
    lift(co_ref, up_ref, order, h1_of, h2_of, mask_to(rows), wanted, ring)
    second_conv(h2_of, h3_of, [i for i in range(half) if not 3 <= i < half - 3], w_ref.at[1], ring, own, c1)

    spread = jnp.transpose(jnp.broadcast_to(outp_ref[...].astype(F32), (128, c1)))
    lane = lax.broadcasted_iota(jnp.int32, (c1, 128), 1)
    pick = jnp.concatenate([jnp.where(lane == r, spread, 0.0).astype(BF16) for r in range(rows)], axis=0)
    parts = []
    for q in range(2):
        found = [h3_of(r) for r in range(rows)]
        parts.append(jnp.concatenate([ref[q, at] for ref, at in found], axis=1))
    sums = jnp.dot(jnp.concatenate(parts, axis=0), pick, preferred_element_type=F32)
    for q in range(2):
        flat_ref[pl.ds(q, own, stride=2), :] = sums[q * own : (q + 1) * own]
    network = jnp.transpose(flat_ref[...])[:rows]

    level = jnp.full((1, 128), now_ref[0], F32)
    after = jnp.full((1, 128), next_ref[0], F32)
    scale_in = 1.0 / jnp.sqrt(level * level + 1.0)
    scale_skip = (1.0 / (level * level + 1.0))[:, :1]
    scale_out = (level * scale_in)[:, :1]
    ratio = (after / level)[:, :1]
    spread_by = jnp.sqrt(level * level - after * after)[:, :1]
    here = pl.ds(pl.multiple_of(place.piece * 2 * own, 128), 2 * own)
    noisy = noisy_ref[:, here]
    denoised = scale_skip * noisy + scale_out * network
    out_ref[...] = denoised + ratio * (noisy - denoised) + spread_by * noise_ref[:, here]


def near(*arrays):
    return [pltpu.with_memory_space_constraint(a, pltpu.VMEM) for a in arrays]


def per_device(
    sizes,
    noisy_field, noise_draw, cond_features, sigma_now, sigma_next, field_proj,
    fine_kernels, coarse_kernel, down_proj, up_proj, out_proj,
):
    rows, cols, c1 = cond_features.shape
    c2 = down_proj.shape[1]
    patches, copies = sizes["patch"], sizes["fsdp"]
    pieces = 2 if copies % 2 == 0 and cols % 256 == 0 else 1
    if sizes["sub"] != 2 or rows < 16:
        raise ValueError("unsupported split")
    window = cols // pieces
    own = window // 2
    ring = own + EDGE
    half = rows // 2
    smem = pl.BlockSpec(memory_space=pltpu.SMEM)
    vmem = pl.BlockSpec(memory_space=pltpu.VMEM)
    where = dict(sizes=sizes, pieces=pieces)
    limit = lambda mib: pltpu.CompilerParams(vmem_limit_bytes=mib << 20)

    mine, tile, send = pl.pallas_call(
        functools.partial(embed_kernel, **where),
        out_shape=[
            pltpu.VMEM((rows, 2, own, c1), BF16),
            pltpu.VMEM((rows, 2, EDGE, c1), BF16),
            pltpu.VMEM((rows, 2, PER, c1), BF16),
        ],
        in_specs=[smem] + [pl.BlockSpec(memory_space=pltpu.HBM)] * 3,
        out_specs=[vmem] * 3,
        scratch_shapes=[
            pltpu.VMEM((rows, window, c1), BF16),
            pltpu.VMEM((rows, EDGE, c1), BF16),
            pltpu.VMEM((rows, EDGE, c1), BF16),
            pltpu.VMEM((rows, cols), F32),
            pltpu.VMEM((1, c1), F32),
            pltpu.VMEM((cols, 128), F32),
            pltpu.VMEM((2, window, c1), F32),
            pltpu.VMEM((2, 2 * EDGE, c1), F32),
            pltpu.SemaphoreType.DMA((5,)),
        ],
        compiler_params=limit(8),
        name="embed",
    )(sigma_now, *[pltpu.with_memory_space_constraint(a, pltpu.HBM) for a in (cond_features, noisy_field, field_proj[None])])

    got = lax.ppermute(send, "sub", [(0, 1), (1, 0)])

    full, upward, downward = pl.pallas_call(
        functools.partial(border_kernel, **where),
        out_shape=[
            pltpu.VMEM((rows, 2, EDGE, c1), BF16),
            pltpu.VMEM((HALO, 2, ring, c1), BF16),
            pltpu.VMEM((HALO, 2, ring, c1), BF16),
        ],
        in_specs=[vmem] * 3,
        out_specs=[vmem] * 3,
        compiler_params=limit(4),
        name="border",
    )(*near(mine, tile, got))

    top = lax.ppermute(upward, "patch", [(i, i + 1) for i in range(patches - 1)])
    bot = lax.ppermute(downward, "patch", [(i + 1, i) for i in range(patches - 1)])

    weights = near(coarse_kernel.reshape(9 * c2, c2), down_proj, up_proj)
    work = 2 * ring * c1 * c1 * 18 * 2 * (half - 2) + 2 * ring * 9 * c2 * c2 * (half - 4)
    inner = pl.pallas_call(
        functools.partial(inner_kernel, **where),
        out_shape=[
            pltpu.VMEM((rows, 4, ring, c1), BF16),
            pltpu.VMEM((2, 12 * c1, 2 * c1), BF16),
            pltpu.VMEM((rows - 4, 2, ring, c1), BF16),
            pltpu.VMEM((half - 2, 3, ring, c2), BF16),
            pltpu.VMEM((rows - 8, 4, ring, c1), BF16),
            pltpu.VMEM((2, rows - 12, own, c1), BF16),
        ],
        in_specs=[vmem] * 6,
        out_specs=[vmem] * 6,
        scratch_shapes=[
            pltpu.VMEM(((half - 2) * ring, c1), BF16),
            pltpu.VMEM(((half - 4) * ring, c2), BF16),
        ],
        cost_estimate=pl.CostEstimate(flops=work * 2, bytes_accessed=4 << 20, transcendentals=0),
        compiler_params=limit(12),
        name="inner",
    )(*near(mine, full, fine_kernels), *weights)

    part = pl.pallas_call(
        functools.partial(outer_kernel, **where),
        out_shape=pltpu.VMEM((rows, window), F32),
        in_specs=[smem, smem] + [vmem] * 14,
        out_specs=vmem,
        scratch_shapes=[
            pltpu.VMEM((2 * HALO, 4, ring, c1), BF16),
            pltpu.VMEM((6 * ring, c1), BF16),
            pltpu.VMEM((6, 2, ring, c1), BF16),
            pltpu.VMEM((6, 3, ring, c2), BF16),
            pltpu.VMEM((6 * ring, c2), BF16),
            pltpu.VMEM((10, 4, ring, c1), BF16),
            pltpu.VMEM((2, 12, own, c1), BF16),
            pltpu.VMEM((window, 128), F32),
        ],
        compiler_params=limit(16),
        name="outer",
    )(sigma_now, sigma_next, *near(top, bot, *inner), *weights, *near(out_proj[None], noisy_field, noise_draw))
    if pieces == 1:
        return part
    other = lax.ppermute(part, "fsdp", [(i, i ^ 1) for i in range(copies)])
    first = lax.rem(lax.axis_index("fsdp"), pieces) == 0
    return jnp.where(first, jnp.concatenate([part, other], axis=1), jnp.concatenate([other, part], axis=1))


def solution(mesh):
    return jax.shard_map(
        functools.partial(per_device, dict(mesh.shape)),
        mesh=mesh,
        in_specs=(
            P(("groups", "patch"), "sub"),
            P(("groups", "patch"), "sub"),
            P(("groups", "patch"), "sub", None),
            P(),
            P(),
            P(),
            P(),
            P(),
            P(),
            P(),
            P(),
        ),
        out_specs=P(("groups", "patch"), "sub"),
        check_vma=False,
    )
```

time: 78 us -> 25.6 us (0.33); the launches traced: 76.9 us -> 25.3 us
  matrix products: 30 us -> 0 us
  starting transfers between devices: 24.9 us -> 8.21 us
  Pallas kernels: 0 us -> 7.98 us
  other arithmetic: 6.41 us -> 0.61 us
  waiting for transfers between devices: 11.5 us -> 5.93 us
  local copies, waits for them, and re-layouts: 2.21 us -> 1.08 us
    dot_general x28 -> x0, matrix products: 30 us -> none  [the longest x26 25.8 us: tap_sum(): jnp.einsum('rci,io->rco', window, kernel[kernel_tap], preferred_element_t...]
    ppermute x12 -> x4, starting transfers between devices: 24.9 us -> 8.21 us  [the longest x1 4.83 us: per_device(): lax.ppermute(upward, 'patch', [(i, i + 1) for i in range(patches - 1)])]
    pallas_call x0 -> x4, Pallas kernels: none -> 7.98 us  [the longest x1 3.43 us: per_device(): pl.pallas_call(functools.partial(outer_kernel, **where), out_shape=pltpu....]
    ppermute x12 -> x4, waiting for transfers between devices: 11.5 us -> 5.93 us  [the longest x1 2.87 us: per_device(): lax.ppermute(downward, 'patch', [(i + 1, i) for i in range(patches - 1)])]
    convert_element_type x3 -> x0, other arithmetic: 2.03 us -> none  [the longest x1 1.76 us: per_device(): hidden0 = (cond_features.astype(jnp.float32) + (scale_in * noisy_field)[:...]
    broadcast_in_dim x2 -> x0, local copies, waits for them, and re-layouts: 1.87 us -> none  [per_device(): lifted = jnp.repeat(jnp.repeat(lifted, 2, axis=0), 2, axis=1)]
    reduce_sum x1 -> x0, other arithmetic: 1.51 us -> none  [per_device(): pooled = hidden1.astype(jnp.float32).reshape(height // 2, 2, breadth // 2...]
    concatenate x3 -> x0, other arithmetic: 1.48 us -> none  [padded_2(): jnp.concatenate([lax.ppermute(tail, axis, [(i, (i + 1) % count) for i in...]
  transfers between devices with their start and end apart: 12 -> 4, of which waited for: 6 -> 3; matrix products, arithmetic and copies ran while one was open for 12% -> 0% of each run, Pallas kernels for 0% -> 11%
where the time goes in v3:
time: 25.6 us; the launch traced here: 25.3 us
  starting transfers between devices  8.21 us (32%)
  Pallas kernels  7.98 us (31%)
  waiting for transfers between devices  5.93 us (23%)
  between operations  1.49 us (6%)
  local copies, waits for them, and re-layouts  1.08 us (4%)
  other arithmetic  0.61 us (2%)
    ppermute x1, starting transfers between devices, per_device(): lax.ppermute(upward, 'patch', [(i, i + 1) for i in range(patches - 1)])  4.83 us
    pallas_call x1, Pallas kernels, per_device(): pl.pallas_call(functools.partial(outer_kernel, **where), out_shape=pltpu....  3.43 us
    ppermute x1, waiting for transfers between devices, per_device(): lax.ppermute(downward, 'patch', [(i + 1, i) for i in range(patches - 1)])  2.87 us
    pallas_call x1, Pallas kernels, per_device(): pl.pallas_call(functools.partial(inner_kernel, **where), out_shape=[pltpu...  2.81 us
    ppermute x1, waiting for transfers between devices, per_device(): other = lax.ppermute(part, 'fsdp', [(i, i ^ 1) for i in range(copies)])  2.16 us
    pallas_call x1, Pallas kernels, per_device(): pl.pallas_call(functools.partial(embed_kernel, **where), out_shape=[pltpu...  1.67 us
    ppermute x1, starting transfers between devices, per_device(): other = lax.ppermute(part, 'fsdp', [(i, i ^ 1) for i in range(copies)])  1.53 us
    ppermute x1, starting transfers between devices, per_device(): lax.ppermute(downward, 'patch', [(i + 1, i) for i in range(patches - 1)])  1.29 us
  transfers between devices with their start and end apart: 4, of which 3 were waited for; matrix products, arithmetic and copies ran while one was open for 0% of the time, Pallas kernels for 11%

profile of v3, /device:TPU:0, one launch (start us, length us, event | category | flops | bytes accessed | tf_op | source)
XLA Modules:
  0.0 25.3 jit_solution(9203406936115120183)
XLA Ops:
  0.0 0.0 copy-start
  0.0 0.0 copy-start.1
  0.0 0.0 copy-start.2
  0.8 1.7 %embed.1 = (bf16[16,2,64,128]{3,2,1,0:T(8,128)(2,1)S(1)}, bf16[16,2,16,128]{3,2,1,0:T(8,128)(2,1)S(1)}, bf16[16,2,8,128]{3,2,1,0:T(8,128)(2,1)S(1)}) custom-call(f32[1]{0:T(128)S(6)} %copy.12.now_ref, bf16[16,256,128]{2,1,0:T(8,128)(2,1)} %cond_ref.1, f32[16,256]{1,0:T(8,128)} %noisy_ref.3, f32[1,128]{1,0:T(1,128)} %bitcast.6), custom_call_target="tpu_custom_call" | custom-call | tf_op jit(solution)/shard_map/embed/pallas_call | solution.py:331
  2.4 0.6 %collective-permute-start = (bf16[16,2,8,128]{3,2,1,0:T(8,128)(2,1)S(1)}, bf16[16,2,8,128]{3,2,1,0:T(8,128)(2,1)S(1)}, u32[]{:S(2)}, u32[]{:S(2)}) collective-permute-start(bf16[16,2,8,128]{3,2,1,0:T(8,128)(2,1)S(1)} %get-tuple-element.19), channel_id=1, source_target_pairs={{0,1},{1,0},{2,3},{3,2},{4,5},{5,4},{6,7},{7,6},{8,9},{9,8},{10,11... | collective-permute-start | bytes 196616 | tf_op jit(solution)/shard_map/ppermute | solution.py:355
  3.0 0.9 %collective-permute-done.got_ref = bf16[16,2,8,128]{3,2,1,0:T(8,128)(2,1)S(1)} collective-permute-done((bf16[16,2,8,128]{3,2,1,0:T(8,128)(2,1)S(1)}, bf16[16,2,8,128]{3,2,1,0:T(8,128)(2,1)S(1)}, u32[]{:S(2)}, u32[]{:S(2)}) %collective-permute-start) | collective-permute-done | bytes 65568 | tf_op jit(solution)/shard_map/ppermute | solution.py:355
  3.9 0.1 border.1
  4.0 4.8 %collective-permute-start.1 = (bf16[5,2,80,128]{3,2,1,0:T(8,128)(2,1)S(1)}, bf16[5,2,80,128]{3,2,1,0:T(8,128)(2,1)S(1)}, u32[]{:S(2)}, u32[]{:S(2)}) collective-permute-start(bf16[5,2,80,128]{3,2,1,0:T(8,128)(2,1)S(1)} %get-tuple-element.20), channel_id=1, source_target_pairs={{0,4},{4,8},{8,12},{1,5},{5,9},{9,13},{2,6},{6,10},{10,14},{3,7},{... | collective-permute-start | bytes 614408 | tf_op jit(solution)/shard_map/ppermute | solution.py:370
  8.8 1.3 %collective-permute-start.2 = (bf16[5,2,80,128]{3,2,1,0:T(8,128)(2,1)S(1)}, bf16[5,2,80,128]{3,2,1,0:T(8,128)(2,1)S(1)}, u32[]{:S(2)}, u32[]{:S(2)}) collective-permute-start(bf16[5,2,80,128]{3,2,1,0:T(8,128)(2,1)S(1)} %get-tuple-element.21), channel_id=1, source_target_pairs={{4,0},{8,4},{12,8},{5,1},{9,5},{13,9},{6,2},{10,6},{14,10},{7,3},{... | collective-permute-start | bytes 614408 | tf_op jit(solution)/shard_map/ppermute | solution.py:371
  10.8 0.0 copy-done
  10.8 0.0 copy-done.1
  10.8 0.0 copy-done.2
  10.8 0.0 copy-start.6
  10.8 1.1 %copy-done.6 = bf16[2,9,128,128]{3,2,1,0:T(8,128)(2,1)S(1)} copy-done((bf16[2,9,128,128]{3,2,1,0:T(8,128)(2,1)S(1)}, bf16[2,9,128,128]{3,2,1,0:T(8,128)(2,1)}, u32[]{:S(2)}) %copy-start.6) | copy-done | bytes 589848
  11.8 0.0 copy-start.3
  11.9 0.0 copy-start.4
  11.9 0.0 copy-start.5
  11.9 2.8 %inner.1 = (bf16[16,4,80,128]{3,2,1,0:T(8,128)(2,1)S(1)}, bf16[2,1536,256]{2,1,0:T(8,128)(2,1)S(1)}, bf16[12,2,80,128]{3,2,1,0:T(8,128)(2,1)S(1)}, bf16[6,3,80,2...) custom-call(bf16[16,2,64,128]{3,2,1,0:T(8,128)(2,1)S(1)} %get-tuple-element.17.mine_, ...), custom_call_target="tpu_custom_call" | custom-call | flops 1887436800 | bytes 4194304 | tf_op jit(solution)/shard_map/inner/pallas_call | solution.py:375
  14.7 0.0 collective-permute-done.1.top_ref
  14.7 2.9 %collective-permute-done.2.bot_ref = bf16[5,2,80,128]{3,2,1,0:T(8,128)(2,1)S(1)} collective-permute-done((bf16[5,2,80,128]{3,2,1,0:T(8,128)(2,1)S(1)}, bf16[5,2,80,128]{3,2,1,0:T(8,128)(2,1)S(1)}, u32[]{:S(2)}, u32[]{:S(2)}) %collective-permute-start.2) | collective-permute-done | bytes 204832 | tf_op jit(solution)/shard_map/ppermute | solution.py:371
  17.6 0.0 copy-done.3
  17.6 0.0 copy-done.4
  17.6 0.0 copy-done.5
  17.6 3.4 %outer.1 = f32[16,128]{1,0:T(8,128)S(1)} custom-call(f32[1]{0:T(128)S(6)} %copy.12.now_ref, f32[1]{0:T(128)S(6)} %copy.13.next_ref, bf16[5,2,80,128]{3,2,1,0:T(8,128)(2,1)S(1)} %collective-permute-done.1.top_ref, bf16[5,2,80,128]{3,2,1,0:T(8,128)(2,1)S(1)} %collective-permute-done.2.bot_ref, bf16[16,4,80,128]{3,2,1,0:T(8,128)(2,1)S(1)} %get-tuple-element.23.xin_ref, ...), custom_call_target="tpu_custom_call" | custom-call | tf_op jit(solution)/shard_map/outer/pallas_call | solution.py:396
  21.0 1.5 %collective-permute-start.3 = (f32[16,128]{1,0:T(8,128)S(1)}, f32[16,128]{1,0:T(8,128)S(1)}, u32[]{:S(2)}, u32[]{:S(2)}) collective-permute-start(f32[16,128]{1,0:T(8,128)S(1)} %outer.1), channel_id=1, source_target_pairs={{0,2},{2,0},{1,3},{3,1},{4,6},{6,4},{5,7},{7,5},{8,10},{10,8},{9,1... | collective-permute-start | bytes 24584 | tf_op jit(solution)/shard_map/ppermute | solution.py:416
  22.5 2.2 %collective-permute-done.3 = f32[16,128]{1,0:T(8,128)S(1)} collective-permute-done((f32[16,128]{1,0:T(8,128)S(1)}, f32[16,128]{1,0:T(8,128)S(1)}, u32[]{:S(2)}, u32[]{:S(2)}) %collective-permute-start.3) | collective-permute-done | bytes 8224 | tf_op jit(solution)/shard_map/ppermute | solution.py:416
  24.7 0.6 %maximum_select_fusion = f32[16,256]{1,0:T(8,128)} fusion(f32[16,128]{1,0:T(8,128)S(1)} %collective-permute-done.3, f32[16,128]{1,0:T(8,128)S(1)} %outer.1, pred[]{:T(512)S(6)} %eq.3), kind=kLoop, calls=%fused_computation | loop fusion | flops 12288 | bytes 32769 | tf_op jit(solution)/shard_map/jit(_where)/select_n | solution.py:418
Async XLA Ops:
  0.0 10.8 %copy-start = (bf16[9,256,256]{2,1,0:T(8,128)(2,1)S(1)}, bf16[9,256,256]{2,1,0:T(8,128)(2,1)}, u32[]{:S(2)}) copy-start(bf16[9,256,256]{2,1,0:T(8,128)(2,1)} %param.18) | copy-start | bytes 3538948
  0.0 10.8 %copy-start.1 = (bf16[128,256]{1,0:T(8,128)(2,1)S(1)}, bf16[128,256]{1,0:T(8,128)(2,1)}, u32[]{:S(2)}) copy-start(bf16[128,256]{1,0:T(8,128)(2,1)} %down_ref.3) | copy-start | bytes 196612
  0.0 10.8 %copy-start.2 = (bf16[256,128]{1,0:T(8,128)(2,1)S(1)}, bf16[256,128]{1,0:T(8,128)(2,1)}, u32[]{:S(2)}) copy-start(bf16[256,128]{1,0:T(8,128)(2,1)} %up_ref.3) | copy-start | bytes 196612
  2.4 1.5 %collective-permute-start = (bf16[16,2,8,128]{3,2,1,0:T(8,128)(2,1)S(1)}, bf16[16,2,8,128]{3,2,1,0:T(8,128)(2,1)S(1)}, u32[]{:S(2)}, u32[]{:S(2)}) collective-permute-start(bf16[16,2,8,128]{3,2,1,0:T(8,128)(2,1)S(1)} %get-tuple-element.19), channel_id=1, source_target_pairs={{0,1},{1,0},{2,3},{3,2},{4,5},{5,4},{6,7},{7,6},{8,9},{9,8},{10,11... | collective-permute-start | bytes 196616 | tf_op jit(solution)/shard_map/ppermute | solution.py:355
  4.0 10.7 %collective-permute-start.1 = (bf16[5,2,80,128]{3,2,1,0:T(8,128)(2,1)S(1)}, bf16[5,2,80,128]{3,2,1,0:T(8,128)(2,1)S(1)}, u32[]{:S(2)}, u32[]{:S(2)}) collective-permute-start(bf16[5,2,80,128]{3,2,1,0:T(8,128)(2,1)S(1)} %get-tuple-element.20), channel_id=1, source_target_pairs={{0,4},{4,8},{8,12},{1,5},{5,9},{9,13},{2,6},{6,10},{10,14},{3,7},{... | collective-permute-start | bytes 614408 | tf_op jit(solution)/shard_map/ppermute | solution.py:370
  8.8 8.8 %collective-permute-start.2 = (bf16[5,2,80,128]{3,2,1,0:T(8,128)(2,1)S(1)}, bf16[5,2,80,128]{3,2,1,0:T(8,128)(2,1)S(1)}, u32[]{:S(2)}, u32[]{:S(2)}) collective-permute-start(bf16[5,2,80,128]{3,2,1,0:T(8,128)(2,1)S(1)} %get-tuple-element.21), channel_id=1, source_target_pairs={{4,0},{8,4},{12,8},{5,1},{9,5},{13,9},{6,2},{10,6},{14,10},{7,3},{... | collective-permute-start | bytes 614408 | tf_op jit(solution)/shard_map/ppermute | solution.py:371
  10.8 1.1 %copy-start.6 = (bf16[2,9,128,128]{3,2,1,0:T(8,128)(2,1)S(1)}, bf16[2,9,128,128]{3,2,1,0:T(8,128)(2,1)}, u32[]{:S(2)}) copy-start(bf16[2,9,128,128]{3,2,1,0:T(8,128)(2,1)} %fine_ref.1) | copy-start | bytes 1769476
  11.8 5.7 %copy-start.3 = (f32[16,256]{1,0:T(8,128)S(1)}, f32[16,256]{1,0:T(8,128)}, u32[]{:S(2)}) copy-start(f32[16,256]{1,0:T(8,128)} %noisy_ref.3) | copy-start | bytes 49156
  11.9 5.7 %copy-start.4 = (f32[16,256]{1,0:T(8,128)S(1)}, f32[16,256]{1,0:T(8,128)}, u32[]{:S(2)}) copy-start(f32[16,256]{1,0:T(8,128)} %noise_ref.1) | copy-start | bytes 49156
  11.9 5.7 %copy-start.5 = (bf16[128]{0:T(256)(128)(2,1)S(1)}, bf16[128]{0:T(256)(128)(2,1)}, u32[]{:S(2)}) copy-start(bf16[128]{0:T(256)(128)(2,1)} %param.21) | copy-start | bytes 772
  21.0 3.7 %collective-permute-start.3 = (f32[16,128]{1,0:T(8,128)S(1)}, f32[16,128]{1,0:T(8,128)S(1)}, u32[]{:S(2)}, u32[]{:S(2)}) collective-permute-start(f32[16,128]{1,0:T(8,128)S(1)} %outer.1), channel_id=1, source_target_pairs={{0,2},{2,0},{1,3},{3,1},{4,6},{6,4},{5,7},{7,5},{8,10},{10,8},{9,1... | collective-permute-start | bytes 24584 | tf_op jit(solution)/shard_map/ppermute | solution.py:416

commit v4 on v3

--- a/solution.py
+++ b/solution.py
@@ -61,11 +61,11 @@
     copies.append(pltpu.make_async_copy(cond_ref.at[:, pl.ds(start, window)], main, sems.at[2]))
     for copy in small + copies:
         copy.start()
-    level = jnp.full((1, 128), now_ref[0], F32)
-    scale_in = 1.0 / jnp.sqrt(level * level + 1.0)
     for copy in small:
         copy.wait()
-    turned[:, :rows] = jnp.transpose(field[...] * scale_in[:, :1])
+    level = now_ref[...]
+    scale_in = 1.0 / jnp.sqrt(level * level + 1.0)
+    turned[:, :rows] = jnp.transpose(field[...] * scale_in)
     proj = embedding[...]
 
     def hidden(buf, r, at):
@@ -93,21 +93,23 @@
             mine_ref[r, q] = wide[r % 2, pl.ds(q, window // 2, stride=2), :].astype(BF16)
 
 
-def border_kernel(mine_ref, tile_ref, got_ref, full_ref, up_ref, down_ref, *, sizes, pieces):
+def border_kernel(mine_ref, tile_ref, got_ref, full_ref, even_ref, odd_ref, brief, *, sizes, pieces):
     rows, _, own, _ = mine_ref.shape
     place = Place(sizes, pieces)
     right = flag(jnp.logical_and(place.last, place.has_right))
     left = flag(jnp.logical_and(place.first, place.has_left))
+    head = lax.broadcasted_iota(jnp.int32, (PER, 128), 0) < PER // 2
     for r in range(rows):
         for q in range(2):
             got = got_ref[r, q].astype(F32)
             tile = tile_ref[r, q].astype(F32) + jnp.concatenate([got * right, got * left], axis=0)
-            tile = tile.astype(BF16)
-            full_ref[r, q] = tile
-            for ref, at in ((down_ref, r), (up_ref, r - rows + HALO)):
-                if 0 <= at < HALO:
-                    ref[at, q, :own] = mine_ref[r, q]
-                    ref[at, q, own:] = tile
+            full_ref[r, q] = tile.astype(BF16)
+            brief[r, q] = jnp.where(head, tile[:PER], tile[PER:]).astype(BF16)
+    low = lax.rem(place.patch, 2) == 0
+    for ref, start in ((even_ref, jnp.where(low, rows - HALO, 0)), (odd_ref, jnp.where(low, 0, rows - HALO))):
+        for n in range(HALO):
+            ref[n, :, :own] = mine_ref[start + n]
+            ref[n, :, own:] = brief[start + n]
 
 
 def put_planes(ref, at, even, odd):
@@ -122,18 +124,18 @@
     return [rows_of[k : k + CHUNK] for k in range(0, len(rows_of), CHUNK)]
 
 
-def conv_pairs(planes_of, pairs, weight):
+def conv_pairs(planes_of, pairs, weight, kept):
     parts = []
     for i in pairs:
         found = [planes_of(2 * i - 1 + d) for d in range(4)]
         for planes in ((2, 0, 1), (0, 1, 3)):
-            parts.append(jnp.concatenate([ref[at, k] for k in planes for ref, at in found], axis=1))
+            parts.append(jnp.concatenate([ref[at, k, :kept] for k in planes for ref, at in found], axis=1))
     return jnp.dot(jnp.concatenate(parts, axis=0), weight[...], preferred_element_type=F32)
 
 
 def first_conv(planes_of, h1_of, pool_ref, slot_of, pairs, weight, ring, c1):
     for group in chunks(pairs):
-        acc = conv_pairs(planes_of, group, weight)
+        acc = conv_pairs(planes_of, group, weight, ring)
         for n, i in enumerate(group):
             total = None
             for o in range(2):
@@ -184,27 +186,20 @@
                 put_planes(into, slot, (ref[at, 0].astype(F32) + lifted) * mask, (ref[at, 1].astype(F32) + lifted) * mask)
 
 
-def second_conv(h2_of, h3_of, pairs, weight, ring, own, c1):
+def second_conv(h2_of, h3_of, pairs, weight, own, c1):
     for group in chunks(pairs):
-        acc = conv_pairs(h2_of, group, weight)
+        acc = conv_pairs(h2_of, group, weight, own)
         for n, i in enumerate(group):
             for o in range(2):
                 ref, at = h2_of(2 * i + o)
                 into, slot = h3_of(2 * i + o)
                 for q in range(2):
-                    v = acc[(2 * n + q) * ring : (2 * n + q) * ring + own, o * c1 : (o + 1) * c1]
+                    v = acc[(2 * n + q) * own : (2 * n + q + 1) * own, o * c1 : (o + 1) * c1]
                     into[q, slot] = (ref[at, q, :own].astype(F32) + silu(v)).astype(BF16)
 
 
-def inner_kernel(
-    mine_ref, tile_ref, fine_ref, coarse_ref, down_ref, up_ref,
-    x_ref, w_ref, h1_ref, ci_ref, h2_ref, h3_ref, pool_ref, co_ref, *, sizes, pieces,
-):
-    rows, _, own, c1 = mine_ref.shape
-    ring = own + EDGE
-    c2 = down_ref.shape[1]
-    half = rows // 2
-    mask = Place(sizes, pieces).column_mask(ring, own)
+def pack_kernel(fine_ref, w_ref):
+    c1 = fine_ref.shape[3]
     for layer in range(2):
         for b in range(3):
             for d in range(4):
@@ -213,6 +208,17 @@
                     a = d - o
                     block = fine_ref[layer, a * 3 + b] if 0 <= a <= 2 else jnp.zeros((c1, c1), BF16)
                     w_ref[layer, at : at + c1, o * c1 : (o + 1) * c1] = block
+
+
+def inner_kernel(
+    mine_ref, tile_ref, w_ref, coarse_ref, down_ref, up_ref,
+    x_ref, h1_ref, ci_ref, h2_ref, h3_ref, pool_ref, co_ref, *, sizes, pieces,
+):
+    rows, _, own, c1 = mine_ref.shape
+    ring = own + EDGE
+    c2 = down_ref.shape[1]
+    half = rows // 2
+    mask = Place(sizes, pieces).column_mask(ring, own)
     for r in range(rows):
         even, odd = (jnp.concatenate([mine_ref[r, q].astype(F32), tile_ref[r, q].astype(F32)], axis=0) for q in range(2))
         put_planes(x_ref, r, even, odd)
@@ -225,11 +231,11 @@
     coarse_in(pool_ref, down_ref, ci_of, range(1, half - 1), lambda i: mask, ring, c2)
     coarse_conv(ci_of, co_ref, list(range(2, half - 2)), coarse_ref, ring)
     lift(co_ref, up_ref, range(2, half - 2), h1_of, h2_of, lambda r: mask, range(4, rows - 4), ring)
-    second_conv(h2_of, h3_of, list(range(3, half - 3)), w_ref.at[1], ring, own, c1)
+    second_conv(h2_of, h3_of, list(range(3, half - 3)), w_ref.at[1], own, c1)
 
 
 def outer_kernel(
-    now_ref, next_ref, top_ref, bot_ref, xin_ref, w_ref, h1in_ref, ciin_ref, h2in_ref, h3in_ref,
+    now_ref, next_ref, odd_ref, even_ref, xin_ref, w_ref, h1in_ref, ciin_ref, h2in_ref, h3in_ref,
     coarse_ref, down_ref, up_ref, outp_ref, noisy_ref, noise_ref, out_ref,
     x_ref, pool_ref, h1_ref, ci_ref, co_ref, h2_ref, h3_ref, flat_ref, *, sizes, pieces,
 ):
@@ -243,9 +249,17 @@
     def mask_to(extent):
         return lambda r: inside * place.above if r < 0 else inside * place.below if r >= extent else inside
 
+    low = lax.rem(place.patch, 2) == 0
+    head = lax.broadcasted_iota(jnp.int32, (PER, 128), 0) < PER // 2
     for n in range(HALO):
-        put_planes(x_ref, n, top_ref[n, 0].astype(F32), top_ref[n, 1].astype(F32))
-        put_planes(x_ref, HALO + n, bot_ref[n, 0].astype(F32), bot_ref[n, 1].astype(F32))
+        above, below = [], []
+        for q in range(2):
+            by_odd, by_even = odd_ref[n, q].astype(F32), even_ref[n, q].astype(F32)
+            for into, v in ((above, jnp.where(low, by_odd, by_even)), (below, jnp.where(low, by_even, by_odd))):
+                edge = v[own:]
+                into.append(jnp.concatenate([v[:own], jnp.where(head, edge, 0.0), jnp.where(head, 0.0, edge)], axis=0))
+        put_planes(x_ref, n, *above)
+        put_planes(x_ref, HALO + n, *below)
 
     def x_of(r):
         return (x_ref, r + HALO) if r < 0 else (xin_ref, r) if r < rows else (x_ref, HALO + r - rows)
@@ -277,7 +291,7 @@
     coarse_conv(ci_of, co_ref, order, coarse_ref, ring)
     wanted = [r for r in range(-1, rows + 1) if not 4 <= r < rows - 4]
     lift(co_ref, up_ref, order, h1_of, h2_of, mask_to(rows), wanted, ring)
-    second_conv(h2_of, h3_of, [i for i in range(half) if not 3 <= i < half - 3], w_ref.at[1], ring, own, c1)
+    second_conv(h2_of, h3_of, [i for i in range(half) if not 3 <= i < half - 3], w_ref.at[1], own, c1)
 
     spread = jnp.transpose(jnp.broadcast_to(outp_ref[...].astype(F32), (128, c1)))
     lane = lax.broadcasted_iota(jnp.int32, (c1, 128), 1)
@@ -291,13 +305,13 @@
         flat_ref[pl.ds(q, own, stride=2), :] = sums[q * own : (q + 1) * own]
     network = jnp.transpose(flat_ref[...])[:rows]
 
-    level = jnp.full((1, 128), now_ref[0], F32)
-    after = jnp.full((1, 128), next_ref[0], F32)
+    level = now_ref[...]
+    after = next_ref[...]
     scale_in = 1.0 / jnp.sqrt(level * level + 1.0)
-    scale_skip = (1.0 / (level * level + 1.0))[:, :1]
-    scale_out = (level * scale_in)[:, :1]
-    ratio = (after / level)[:, :1]
-    spread_by = jnp.sqrt(level * level - after * after)[:, :1]
+    scale_skip = 1.0 / (level * level + 1.0)
+    scale_out = level * scale_in
+    ratio = after / level
+    spread_by = jnp.sqrt(level * level - after * after)
     here = pl.ds(pl.multiple_of(place.piece * 2 * own, 128), 2 * own)
     noisy = noisy_ref[:, here]
     denoised = scale_skip * noisy + scale_out * network
@@ -323,7 +337,6 @@
     own = window // 2
     ring = own + EDGE
     half = rows // 2
-    smem = pl.BlockSpec(memory_space=pltpu.SMEM)
     vmem = pl.BlockSpec(memory_space=pltpu.VMEM)
     where = dict(sizes=sizes, pieces=pieces)
     limit = lambda mib: pltpu.CompilerParams(vmem_limit_bytes=mib << 20)
@@ -335,7 +348,7 @@
             pltpu.VMEM((rows, 2, EDGE, c1), BF16),
             pltpu.VMEM((rows, 2, PER, c1), BF16),
         ],
-        in_specs=[smem] + [pl.BlockSpec(memory_space=pltpu.HBM)] * 3,
+        in_specs=[vmem] + [pl.BlockSpec(memory_space=pltpu.HBM)] * 3,
         out_specs=[vmem] * 3,
         scratch_shapes=[
             pltpu.VMEM((rows, window, c1), BF16),
@@ -350,25 +363,39 @@
         ],
         compiler_params=limit(8),
         name="embed",
-    )(sigma_now, *[pltpu.with_memory_space_constraint(a, pltpu.HBM) for a in (cond_features, noisy_field, field_proj[None])])
+    )(sigma_now[None], *[pltpu.with_memory_space_constraint(a, pltpu.HBM) for a in (cond_features, noisy_field, field_proj[None])])
 
     got = lax.ppermute(send, "sub", [(0, 1), (1, 0)])
 
-    full, upward, downward = pl.pallas_call(
+    packed = pl.pallas_call(
+        pack_kernel,
+        out_shape=pltpu.VMEM((2, 12 * c1, 2 * c1), BF16),
+        in_specs=[vmem],
+        out_specs=vmem,
+        cost_estimate=pl.CostEstimate(flops=0, bytes_accessed=2 << 20, transcendentals=0),
+        compiler_params=limit(4),
+        name="pack",
+    )(*near(fine_kernels))
+
+    full, for_even, for_odd = pl.pallas_call(
         functools.partial(border_kernel, **where),
         out_shape=[
             pltpu.VMEM((rows, 2, EDGE, c1), BF16),
-            pltpu.VMEM((HALO, 2, ring, c1), BF16),
-            pltpu.VMEM((HALO, 2, ring, c1), BF16),
+            pltpu.VMEM((HALO, 2, own + PER, c1), BF16),
+            pltpu.VMEM((HALO, 2, own + PER, c1), BF16),
         ],
         in_specs=[vmem] * 3,
         out_specs=[vmem] * 3,
+        scratch_shapes=[pltpu.VMEM((rows, 2, PER, c1), BF16)],
         compiler_params=limit(4),
         name="border",
     )(*near(mine, tile, got))
 
-    top = lax.ppermute(upward, "patch", [(i, i + 1) for i in range(patches - 1)])
-    bot = lax.ppermute(downward, "patch", [(i + 1, i) for i in range(patches - 1)])
+    def swap(rows_to_give, low):
+        return lax.ppermute(rows_to_give, "patch", [pair for i in range(low, patches - 1, 2) for pair in ((i, i + 1), (i + 1, i))])
+
+    odd = swap(for_odd, 1)
+    even = swap(for_even, 0)
 
     weights = near(coarse_kernel.reshape(9 * c2, c2), down_proj, up_proj)
     work = 2 * ring * c1 * c1 * 18 * 2 * (half - 2) + 2 * ring * 9 * c2 * c2 * (half - 4)
@@ -376,14 +403,13 @@
         functools.partial(inner_kernel, **where),
         out_shape=[
             pltpu.VMEM((rows, 4, ring, c1), BF16),
-            pltpu.VMEM((2, 12 * c1, 2 * c1), BF16),
             pltpu.VMEM((rows - 4, 2, ring, c1), BF16),
             pltpu.VMEM((half - 2, 3, ring, c2), BF16),
             pltpu.VMEM((rows - 8, 4, ring, c1), BF16),
             pltpu.VMEM((2, rows - 12, own, c1), BF16),
         ],
         in_specs=[vmem] * 6,
-        out_specs=[vmem] * 6,
+        out_specs=[vmem] * 5,
         scratch_shapes=[
             pltpu.VMEM(((half - 2) * ring, c1), BF16),
             pltpu.VMEM(((half - 4) * ring, c2), BF16),
@@ -391,12 +417,12 @@
         cost_estimate=pl.CostEstimate(flops=work * 2, bytes_accessed=4 << 20, transcendentals=0),
         compiler_params=limit(12),
         name="inner",
-    )(*near(mine, full, fine_kernels), *weights)
+    )(*near(mine, full, packed), *weights)
 
     part = pl.pallas_call(
         functools.partial(outer_kernel, **where),
         out_shape=pltpu.VMEM((rows, window), F32),
-        in_specs=[smem, smem] + [vmem] * 14,
+        in_specs=[vmem] * 16,
         out_specs=vmem,
         scratch_shapes=[
             pltpu.VMEM((2 * HALO, 4, ring, c1), BF16),
@@ -410,7 +436,7 @@
         ],
         compiler_params=limit(16),
         name="outer",
-    )(sigma_now, sigma_next, *near(top, bot, *inner), *weights, *near(out_proj[None], noisy_field, noise_draw))
+    )(sigma_now[None], sigma_next[None], *near(odd, even, *inner[:1], packed, *inner[1:]), *weights, *near(out_proj[None], noisy_field, noise_draw))
     if pieces == 1:
         return part
     other = lax.ppermute(part, "fsdp", [(i, i ^ 1) for i in range(copies)])

time: 25.6 us -> 23.1 us (0.902)
  waiting for transfers between devices: 5.93 us -> 4.25 us
  local copies, waits for them, and re-layouts: 1.08 us -> 0.03 us
  starting transfers between devices: 8.21 us -> 8.69 us
    ppermute x2, waiting for transfers between devices: 2.87 us -> 1.2 us  [swap(): lax.ppermute(rows_to_give, 'patch', [pair for i in range(low, patches - 1...]
    unnamed x14, local copies, waits for them, and re-layouts: 1.08 us -> 0.03 us
    ppermute x2, starting transfers between devices: 6.12 us -> 6.59 us  [swap(): lax.ppermute(rows_to_give, 'patch', [pair for i in range(low, patches - 1...]
    pallas_call x1, Pallas kernels: 2.81 us -> 2.54 us  [per_device(): pl.pallas_call(functools.partial(inner_kernel, **where), out_shape=[pltpu...]
  transfers between devices with their start and end apart: 4 -> 4, of which waited for: 3 -> 3; matrix products, arithmetic and copies ran while one was open for 0% -> 0% of each run, Pallas kernels for 11% -> 12%
where the time goes in v4:
time: 23.1 us; the launch traced here: 22.8 us
  starting transfers between devices  8.69 us (38%)
  Pallas kernels  7.75 us (34%)
  waiting for transfers between devices  4.25 us (18%)
  between operations  1.46 us (6%)
  other arithmetic  0.61 us (3%)
    ppermute x2, starting transfers between devices, swap(): lax.ppermute(rows_to_give, 'patch', [pair for i in range(low, patches - 1...  6.59 us
    pallas_call x1, Pallas kernels, per_device(): pl.pallas_call(functools.partial(outer_kernel, **where), out_shape=pltpu....  3.26 us
    pallas_call x1, Pallas kernels, per_device(): pl.pallas_call(functools.partial(inner_kernel, **where), out_shape=[pltpu...  2.54 us
    ppermute x1, waiting for transfers between devices, per_device(): other = lax.ppermute(part, 'fsdp', [(i, i ^ 1) for i in range(copies)])  2.15 us
    pallas_call x1, Pallas kernels, per_device(): pl.pallas_call(functools.partial(embed_kernel, **where), out_shape=[pltpu...  1.67 us
    ppermute x1, starting transfers between devices, per_device(): other = lax.ppermute(part, 'fsdp', [(i, i ^ 1) for i in range(copies)])  1.53 us
    ppermute x2, waiting for transfers between devices, swap(): lax.ppermute(rows_to_give, 'patch', [pair for i in range(low, patches - 1...  1.2 us
    ppermute x1, waiting for transfers between devices, per_device(): got = lax.ppermute(send, 'sub', [(0, 1), (1, 0)])  0.9 us
  transfers between devices with their start and end apart: 4, of which 3 were waited for; matrix products, arithmetic and copies ran while one was open for 0% of the time, Pallas kernels for 12%

profile of v4, /device:TPU:0, one launch (start us, length us, event | category | flops | bytes accessed | tf_op | source)
XLA Modules:
  0.0 22.8 jit_solution(13890080988639600971)
XLA Ops:
  0.0 0.0 copy-start.1
  0.7 1.7 %embed.1 = (bf16[16,2,64,128]{3,2,1,0:T(8,128)(2,1)S(1)}, bf16[16,2,16,128]{3,2,1,0:T(8,128)(2,1)S(1)}, bf16[16,2,8,128]{3,2,1,0:T(8,128)(2,1)S(1)}) custom-call(f32[1,1]{1,0:T(1,128)} %bitcast.5.now_ref, bf16[16,256,128]{2,1,0:T(8,128)(2,1)} %cond_ref.1, f32[16,256]{1,0:T(8,128)} %noisy_ref.3, f32[1,128]{1,0:T(1,128)} %bitcast.11), custom_call_target="tpu_custom_call" | custom-call | tf_op jit(solution)/shard_map/embed/pallas_call | solution.py:344
  2.4 0.6 %collective-permute-start = (bf16[16,2,8,128]{3,2,1,0:T(8,128)(2,1)S(1)}, bf16[16,2,8,128]{3,2,1,0:T(8,128)(2,1)S(1)}, u32[]{:S(2)}, u32[]{:S(2)}) collective-permute-start(bf16[16,2,8,128]{3,2,1,0:T(8,128)(2,1)S(1)} %get-tuple-element.18), channel_id=1, source_target_pairs={{0,1},{1,0},{2,3},{3,2},{4,5},{5,4},{6,7},{7,6},{8,9},{9,8},{10,11... | collective-permute-start | bytes 196616 | tf_op jit(solution)/shard_map/ppermute | solution.py:368
  3.0 0.9 %collective-permute-done.got_ref = bf16[16,2,8,128]{3,2,1,0:T(8,128)(2,1)S(1)} collective-permute-done((bf16[16,2,8,128]{3,2,1,0:T(8,128)(2,1)S(1)}, bf16[16,2,8,128]{3,2,1,0:T(8,128)(2,1)S(1)}, u32[]{:S(2)}, u32[]{:S(2)}) %collective-permute-start) | collective-permute-done | bytes 65568 | tf_op jit(solution)/shard_map/ppermute | solution.py:368
  3.9 0.0 copy-start
  3.9 0.0 copy-start.2
  3.9 0.0 copy-start.3
  3.9 0.1 border.1
  3.9 0.8 %collective-permute-start.1 = (bf16[5,2,72,128]{3,2,1,0:T(8,128)(2,1)S(1)}, bf16[5,2,72,128]{3,2,1,0:T(8,128)(2,1)S(1)}, u32[]{:S(2)}, u32[]{:S(2)}) collective-permute-start(bf16[5,2,72,128]{3,2,1,0:T(8,128)(2,1)S(1)} %get-tuple-element.19), channel_id=1, source_target_pairs={{4,8},{8,4},{5,9},{9,5},{6,10},{10,6},{7,11},{11,7},{20,24},{24,20... | collective-permute-start | bytes 552968 | tf_op jit(solution)/shard_map/ppermute | solution.py:395
  4.8 5.8 %collective-permute-start.2 = (bf16[5,2,72,128]{3,2,1,0:T(8,128)(2,1)S(1)}, bf16[5,2,72,128]{3,2,1,0:T(8,128)(2,1)S(1)}, u32[]{:S(2)}, u32[]{:S(2)}) collective-permute-start(bf16[5,2,72,128]{3,2,1,0:T(8,128)(2,1)S(1)} %get-tuple-element.20), channel_id=1, source_target_pairs={{0,4},{4,0},{8,12},{12,8},{1,5},{5,1},{9,13},{13,9},{2,6},{6,2},{1... | collective-permute-start | bytes 552968 | tf_op jit(solution)/shard_map/ppermute | solution.py:395
  10.5 0.0 copy-done.1
  10.6 0.2 pack.1.w_ref
  11.4 0.0 copy-done
  11.4 0.0 copy-done.2
  11.4 0.0 copy-done.3
  11.4 0.0 copy-start.4
  11.4 0.0 copy-start.5
  11.5 0.0 copy-start.6
  11.5 2.5 %inner.1 = (bf16[16,4,80,128]{3,2,1,0:T(8,128)(2,1)S(1)}, bf16[12,2,80,128]{3,2,1,0:T(8,128)(2,1)S(1)}, bf16[6,3,80,256]{3,2,1,0:T(8,128)(2,1)S(1)}, bf16[8,4,80...) custom-call(bf16[16,2,64,128]{3,2,1,0:T(8,128)(2,1)S(1)} %get-tuple-element.16.mine_ref, ...), custom_call_target="tpu_custom_call" | custom-call | flops 1887436800 | bytes 4194304 | tf_op jit(solution)/shard_map/inner/pallas_call | solution.py:402
  14.0 0.0 collective-permute-done.1.odd_ref
  14.0 1.2 %collective-permute-done.2.even_ref = bf16[5,2,72,128]{3,2,1,0:T(8,128)(2,1)S(1)} collective-permute-done((bf16[5,2,72,128]{3,2,1,0:T(8,128)(2,1)S(1)}, bf16[5,2,72,128]{3,2,1,0:T(8,128)(2,1)S(1)}, u32[]{:S(2)}, u32[]{:S(2)}) %collective-permute-start.2) | collective-permute-done | bytes 184352 | tf_op jit(solution)/shard_map/ppermute | solution.py:395
  15.2 0.0 copy-done.4
  15.2 0.0 copy-done.5
  15.2 0.0 copy-done.6
  15.2 3.3 %outer.1 = f32[16,128]{1,0:T(8,128)S(1)} custom-call(f32[1,1]{1,0:T(1,128)} %bitcast.6.now_ref, f32[1,1]{1,0:T(1,128)} %bitcast.7.next_ref, bf16[5,2,72,128]{3,2,1,0:T(8,128)(2,1)S(1)} %collective-permute-done.1.odd_ref, bf16[5,2,72,128]{3,2,1,0:T(8,128)(2,1)S(1)} %collective-permute-done.2.even_ref, bf16[16,4,80,128]{3,2,1,0:T(8,128)(2,1)S(1)} %get-tuple-element.22.xin_ref, ...), custom_call_target="tpu_custom_call" | custom-call | tf_op jit(solution)/shard_map/outer/pallas_call | solution.py:422
  18.5 1.5 %collective-permute-start.3 = (f32[16,128]{1,0:T(8,128)S(1)}, f32[16,128]{1,0:T(8,128)S(1)}, u32[]{:S(2)}, u32[]{:S(2)}) collective-permute-start(f32[16,128]{1,0:T(8,128)S(1)} %outer.1), channel_id=1, source_target_pairs={{0,2},{2,0},{1,3},{3,1},{4,6},{6,4},{5,7},{7,5},{8,10},{10,8},{9,1... | collective-permute-start | bytes 24584 | tf_op jit(solution)/shard_map/ppermute | solution.py:442
  20.0 2.2 %collective-permute-done.3 = f32[16,128]{1,0:T(8,128)S(1)} collective-permute-done((f32[16,128]{1,0:T(8,128)S(1)}, f32[16,128]{1,0:T(8,128)S(1)}, u32[]{:S(2)}, u32[]{:S(2)}) %collective-permute-start.3) | collective-permute-done | bytes 8224 | tf_op jit(solution)/shard_map/ppermute | solution.py:442
  22.2 0.6 %maximum_select_fusion = f32[16,256]{1,0:T(8,128)} fusion(f32[16,128]{1,0:T(8,128)S(1)} %collective-permute-done.3, f32[16,128]{1,0:T(8,128)S(1)} %outer.1, pred[]{:T(512)S(6)} %eq.3), kind=kLoop, calls=%fused_computation | loop fusion | flops 12288 | bytes 32769 | tf_op jit(solution)/shard_map/jit(_where)/select_n | solution.py:444
Async XLA Ops:
  0.0 10.5 %copy-start.1 = (bf16[2,9,128,128]{3,2,1,0:T(8,128)(2,1)S(1)}, bf16[2,9,128,128]{3,2,1,0:T(8,128)(2,1)}, u32[]{:S(2)}) copy-start(bf16[2,9,128,128]{3,2,1,0:T(8,128)(2,1)} %fine_ref.1) | copy-start | bytes 1769476
  2.4 1.5 %collective-permute-start = (bf16[16,2,8,128]{3,2,1,0:T(8,128)(2,1)S(1)}, bf16[16,2,8,128]{3,2,1,0:T(8,128)(2,1)S(1)}, u32[]{:S(2)}, u32[]{:S(2)}) collective-permute-start(bf16[16,2,8,128]{3,2,1,0:T(8,128)(2,1)S(1)} %get-tuple-element.18), channel_id=1, source_target_pairs={{0,1},{1,0},{2,3},{3,2},{4,5},{5,4},{6,7},{7,6},{8,9},{9,8},{10,11... | collective-permute-start | bytes 196616 | tf_op jit(solution)/shard_map/ppermute | solution.py:368
  3.9 7.5 %copy-start = (bf16[9,256,256]{2,1,0:T(8,128)(2,1)S(1)}, bf16[9,256,256]{2,1,0:T(8,128)(2,1)}, u32[]{:S(2)}) copy-start(bf16[9,256,256]{2,1,0:T(8,128)(2,1)} %param.18) | copy-start | bytes 3538948
  3.9 7.6 %copy-start.2 = (bf16[128,256]{1,0:T(8,128)(2,1)S(1)}, bf16[128,256]{1,0:T(8,128)(2,1)}, u32[]{:S(2)}) copy-start(bf16[128,256]{1,0:T(8,128)(2,1)} %down_ref.3) | copy-start | bytes 196612
  3.9 7.6 %copy-start.3 = (bf16[256,128]{1,0:T(8,128)(2,1)S(1)}, bf16[256,128]{1,0:T(8,128)(2,1)}, u32[]{:S(2)}) copy-start(bf16[256,128]{1,0:T(8,128)(2,1)} %up_ref.3) | copy-start | bytes 196612
  3.9 10.1 %collective-permute-start.1 = (bf16[5,2,72,128]{3,2,1,0:T(8,128)(2,1)S(1)}, bf16[5,2,72,128]{3,2,1,0:T(8,128)(2,1)S(1)}, u32[]{:S(2)}, u32[]{:S(2)}) collective-permute-start(bf16[5,2,72,128]{3,2,1,0:T(8,128)(2,1)S(1)} %get-tuple-element.19), channel_id=1, source_target_pairs={{4,8},{8,4},{5,9},{9,5},{6,10},{10,6},{7,11},{11,7},{20,24},{24,20... | collective-permute-start | bytes 552968 | tf_op jit(solution)/shard_map/ppermute | solution.py:395
  4.8 10.5 %collective-permute-start.2 = (bf16[5,2,72,128]{3,2,1,0:T(8,128)(2,1)S(1)}, bf16[5,2,72,128]{3,2,1,0:T(8,128)(2,1)S(1)}, u32[]{:S(2)}, u32[]{:S(2)}) collective-permute-start(bf16[5,2,72,128]{3,2,1,0:T(8,128)(2,1)S(1)} %get-tuple-element.20), channel_id=1, source_target_pairs={{0,4},{4,0},{8,12},{12,8},{1,5},{5,1},{9,13},{13,9},{2,6},{6,2},{1... | collective-permute-start | bytes 552968 | tf_op jit(solution)/shard_map/ppermute | solution.py:395
  11.4 3.8 %copy-start.4 = (f32[16,256]{1,0:T(8,128)S(1)}, f32[16,256]{1,0:T(8,128)}, u32[]{:S(2)}) copy-start(f32[16,256]{1,0:T(8,128)} %noisy_ref.3) | copy-start | bytes 49156
  11.4 3.8 %copy-start.5 = (f32[16,256]{1,0:T(8,128)S(1)}, f32[16,256]{1,0:T(8,128)}, u32[]{:S(2)}) copy-start(f32[16,256]{1,0:T(8,128)} %noise_ref.1) | copy-start | bytes 49156
  11.5 3.8 %copy-start.6 = (bf16[128]{0:T(256)(128)(2,1)S(1)}, bf16[128]{0:T(256)(128)(2,1)}, u32[]{:S(2)}) copy-start(bf16[128]{0:T(256)(128)(2,1)} %param.21) | copy-start | bytes 772
  18.5 3.7 %collective-permute-start.3 = (f32[16,128]{1,0:T(8,128)S(1)}, f32[16,128]{1,0:T(8,128)S(1)}, u32[]{:S(2)}, u32[]{:S(2)}) collective-permute-start(f32[16,128]{1,0:T(8,128)S(1)} %outer.1), channel_id=1, source_target_pairs={{0,2},{2,0},{1,3},{3,1},{4,6},{6,4},{5,7},{7,5},{8,10},{10,8},{9,1... | collective-permute-start | bytes 24584 | tf_op jit(solution)/shard_map/ppermute | solution.py:442

commit v5 on v4

--- a/solution.py
+++ b/solution.py
@@ -15,9 +15,12 @@
 CHUNK = 3
 
 
+def silu_of_half(half):
+    return half + half * jnp.tanh(half)
+
+
 def silu(v):
-    half = 0.5 * v
-    return half + half * jnp.tanh(half)
+    return silu_of_half(0.5 * v)
 
 
 def flag(condition):
@@ -38,7 +41,7 @@
 
     def column_mask(self, ring, own):
         at = lax.broadcasted_iota(jnp.int32, (ring, 128), 0)
-        return jnp.where(at < own, 1.0, jnp.where(at < own + PER, flag(self.has_right), flag(self.has_left)))
+        return jnp.where(at < own, 1.0, jnp.where(at < own + PER // 2, flag(self.has_right), flag(self.has_left)))
 
 
 def embed_kernel(
@@ -67,6 +70,7 @@
     scale_in = 1.0 / jnp.sqrt(level * level + 1.0)
     turned[:, :rows] = jnp.transpose(field[...] * scale_in)
     proj = embedding[...]
+    head = lax.broadcasted_iota(jnp.int32, (PER, 128), 0) < PER // 2
 
     def hidden(buf, r, at):
         return buf[r].astype(F32) + turned[pl.ds(at, buf.shape[1]), r : r + 1] * proj
@@ -83,7 +87,7 @@
                 block = edge[r % 2, pl.ds(EDGE + q, PER, stride=2), :]
                 to_right = block * flag(jnp.logical_not(place.last))
                 to_left = block * flag(jnp.logical_not(place.first))
-                tile_ref[r, q] = jnp.concatenate([to_right, to_left], axis=0).astype(BF16)
+                tile_ref[r, q] = jnp.where(head, to_right, to_left).astype(BF16)
         else:
             tile_ref[r] = jnp.zeros_like(tile_ref[r])
     copies[-1].wait()
@@ -93,7 +97,7 @@
             mine_ref[r, q] = wide[r % 2, pl.ds(q, window // 2, stride=2), :].astype(BF16)
 
 
-def border_kernel(mine_ref, tile_ref, got_ref, full_ref, even_ref, odd_ref, brief, *, sizes, pieces):
+def border_kernel(mine_ref, tile_ref, got_ref, full_ref, even_ref, odd_ref, *, sizes, pieces):
     rows, _, own, _ = mine_ref.shape
     place = Place(sizes, pieces)
     right = flag(jnp.logical_and(place.last, place.has_right))
@@ -102,14 +106,13 @@
     for r in range(rows):
         for q in range(2):
             got = got_ref[r, q].astype(F32)
-            tile = tile_ref[r, q].astype(F32) + jnp.concatenate([got * right, got * left], axis=0)
+            tile = tile_ref[r, q].astype(F32) + jnp.where(head, got * right, got * left)
             full_ref[r, q] = tile.astype(BF16)
-            brief[r, q] = jnp.where(head, tile[:PER], tile[PER:]).astype(BF16)
     low = lax.rem(place.patch, 2) == 0
     for ref, start in ((even_ref, jnp.where(low, rows - HALO, 0)), (odd_ref, jnp.where(low, 0, rows - HALO))):
         for n in range(HALO):
             ref[n, :, :own] = mine_ref[start + n]
-            ref[n, :, own:] = brief[start + n]
+            ref[n, :, own:] = full_ref[start + n]
 
 
 def put_planes(ref, at, even, odd):
@@ -118,6 +121,13 @@
     ref[at, 1] = odd.astype(BF16)
     ref[at, 2] = pltpu.roll(odd, 1, 0).astype(BF16)
     ref[at, 3] = pltpu.roll(even, ring - 1, 0).astype(BF16)
+
+
+def masked(x, columns, row):
+    own = x.shape[0] - PER
+    columns = jnp.concatenate([columns[own:]] * (x.shape[1] // 128), axis=1)
+    x = jnp.concatenate([x[:own], x[own:] * columns], axis=0)
+    return x if row is None else x * row
 
 
 def chunks(rows_of):
@@ -142,7 +152,7 @@
                 ref, at = planes_of(2 * i + o)
                 for q in range(2):
                     v = acc[(2 * n + q) * ring : (2 * n + q + 1) * ring, o * c1 : (o + 1) * c1]
-                    h = (ref[at, q].astype(F32) + silu(v)).astype(BF16)
+                    h = (ref[at, q].astype(F32) + silu_of_half(v)).astype(BF16)
                     kept = h1_of(2 * i + o)
                     if kept is not None:
                         kept[0][kept[1], q] = h
@@ -153,7 +163,7 @@
 def coarse_in(pool_ref, down_ref, ci_of, order, mask_of, ring, c2):
     ci_all = jnp.dot(pool_ref[...], down_ref[...], preferred_element_type=F32)
     for n, i in enumerate(order):
-        ci = ci_all[n * ring : (n + 1) * ring] * jnp.concatenate([mask_of(i)] * (c2 // 128), axis=1)
+        ci = masked(ci_all[n * ring : (n + 1) * ring], *mask_of(i))
         ref, at = ci_of(i)
         ref[at, 0] = pltpu.roll(ci, 1, 0).astype(BF16)
         ref[at, 1] = ci.astype(BF16)
@@ -183,7 +193,7 @@
                 ref, at = h1_of(r)
                 mask = mask_of(r)
                 into, slot = h2_of(r)
-                put_planes(into, slot, (ref[at, 0].astype(F32) + lifted) * mask, (ref[at, 1].astype(F32) + lifted) * mask)
+                put_planes(into, slot, *(masked(ref[at, q].astype(F32) + lifted, *mask) for q in range(2)))
 
 
 def second_conv(h2_of, h3_of, pairs, weight, own, c1):
@@ -195,7 +205,7 @@
                 into, slot = h3_of(2 * i + o)
                 for q in range(2):
                     v = acc[(2 * n + q) * own : (2 * n + q + 1) * own, o * c1 : (o + 1) * c1]
-                    into[q, slot] = (ref[at, q, :own].astype(F32) + silu(v)).astype(BF16)
+                    into[q, slot] = (ref[at, q, :own].astype(F32) + silu_of_half(v)).astype(BF16)
 
 
 def pack_kernel(fine_ref, w_ref):
@@ -206,7 +216,7 @@
                 at = (b * 4 + d) * c1
                 for o in range(2):
                     a = d - o
-                    block = fine_ref[layer, a * 3 + b] if 0 <= a <= 2 else jnp.zeros((c1, c1), BF16)
+                    block = fine_ref[layer, a * 3 + b] * 0.5 if 0 <= a <= 2 else jnp.zeros((c1, c1), BF16)
                     w_ref[layer, at : at + c1, o * c1 : (o + 1) * c1] = block
 
 
@@ -215,7 +225,7 @@
     x_ref, h1_ref, ci_ref, h2_ref, h3_ref, pool_ref, co_ref, *, sizes, pieces,
 ):
     rows, _, own, c1 = mine_ref.shape
-    ring = own + EDGE
+    ring = own + PER
     c2 = down_ref.shape[1]
     half = rows // 2
     mask = Place(sizes, pieces).column_mask(ring, own)
@@ -228,9 +238,9 @@
     h2_of = lambda r: (h2_ref, r - 4)
     h3_of = lambda r: (h3_ref, r - 6)
     first_conv(x_of, h1_of, pool_ref, lambda i: i - 1, list(range(1, half - 1)), w_ref.at[0], ring, c1)
-    coarse_in(pool_ref, down_ref, ci_of, range(1, half - 1), lambda i: mask, ring, c2)
+    coarse_in(pool_ref, down_ref, ci_of, range(1, half - 1), lambda i: (mask, None), ring, c2)
     coarse_conv(ci_of, co_ref, list(range(2, half - 2)), coarse_ref, ring)
-    lift(co_ref, up_ref, range(2, half - 2), h1_of, h2_of, lambda r: mask, range(4, rows - 4), ring)
+    lift(co_ref, up_ref, range(2, half - 2), h1_of, h2_of, lambda r: (mask, None), range(4, rows - 4), ring)
     second_conv(h2_of, h3_of, list(range(3, half - 3)), w_ref.at[1], own, c1)
 
 
@@ -240,24 +250,22 @@
     x_ref, pool_ref, h1_ref, ci_ref, co_ref, h2_ref, h3_ref, flat_ref, *, sizes, pieces,
 ):
     rows, _, ring, c1 = xin_ref.shape
-    own = ring - EDGE
+    own = ring - PER
     c2 = down_ref.shape[1]
     half = rows // 2
     place = Place(sizes, pieces)
     inside = place.column_mask(ring, own)
 
     def mask_to(extent):
-        return lambda r: inside * place.above if r < 0 else inside * place.below if r >= extent else inside
+        return lambda r: (inside, place.above if r < 0 else place.below if r >= extent else None)
 
     low = lax.rem(place.patch, 2) == 0
-    head = lax.broadcasted_iota(jnp.int32, (PER, 128), 0) < PER // 2
     for n in range(HALO):
         above, below = [], []
         for q in range(2):
             by_odd, by_even = odd_ref[n, q].astype(F32), even_ref[n, q].astype(F32)
-            for into, v in ((above, jnp.where(low, by_odd, by_even)), (below, jnp.where(low, by_even, by_odd))):
-                edge = v[own:]
-                into.append(jnp.concatenate([v[:own], jnp.where(head, edge, 0.0), jnp.where(head, 0.0, edge)], axis=0))
+            above.append(jnp.where(low, by_odd, by_even))
+            below.append(jnp.where(low, by_even, by_odd))
         put_planes(x_ref, n, *above)
         put_planes(x_ref, HALO + n, *below)
 
@@ -335,7 +343,7 @@
         raise ValueError("unsupported split")
     window = cols // pieces
     own = window // 2
-    ring = own + EDGE
+    ring = own + PER
     half = rows // 2
     vmem = pl.BlockSpec(memory_space=pltpu.VMEM)
     where = dict(sizes=sizes, pieces=pieces)
@@ -345,7 +353,7 @@
         functools.partial(embed_kernel, **where),
         out_shape=[
             pltpu.VMEM((rows, 2, own, c1), BF16),
-            pltpu.VMEM((rows, 2, EDGE, c1), BF16),
+            pltpu.VMEM((rows, 2, PER, c1), BF16),
             pltpu.VMEM((rows, 2, PER, c1), BF16),
         ],
         in_specs=[vmem] + [pl.BlockSpec(memory_space=pltpu.HBM)] * 3,
@@ -380,13 +388,12 @@
     full, for_even, for_odd = pl.pallas_call(
         functools.partial(border_kernel, **where),
         out_shape=[
-            pltpu.VMEM((rows, 2, EDGE, c1), BF16),
-            pltpu.VMEM((HALO, 2, own + PER, c1), BF16),
-            pltpu.VMEM((HALO, 2, own + PER, c1), BF16),
+            pltpu.VMEM((rows, 2, PER, c1), BF16),
+            pltpu.VMEM((HALO, 2, ring, c1), BF16),
+            pltpu.VMEM((HALO, 2, ring, c1), BF16),
         ],
         in_specs=[vmem] * 3,
         out_specs=[vmem] * 3,
-        scratch_shapes=[pltpu.VMEM((rows, 2, PER, c1), BF16)],
         compiler_params=limit(4),
         name="border",
     )(*near(mine, tile, got))

time: 23.1 us -> 22.8 us (0.987)
  no operation moved by 1% of the time
where the time goes in v5:
time: 22.8 us; the launch traced here: 22.6 us
  starting transfers between devices  8.68 us (38%)
  Pallas kernels  7.54 us (33%)
  waiting for transfers between devices  4.24 us (19%)
  between operations  1.48 us (6%)
  other arithmetic  0.61 us (3%)
    ppermute x2, starting transfers between devices, swap(): lax.ppermute(rows_to_give, 'patch', [pair for i in range(low, patches - 1...  6.59 us
    pallas_call x1, Pallas kernels, per_device(): pl.pallas_call(functools.partial(outer_kernel, **where), out_shape=pltpu....  3.05 us
    pallas_call x1, Pallas kernels, per_device(): pl.pallas_call(functools.partial(inner_kernel, **where), out_shape=[pltpu...  2.52 us
    ppermute x1, waiting for transfers between devices, per_device(): other = lax.ppermute(part, 'fsdp', [(i, i ^ 1) for i in range(copies)])  2.16 us
    pallas_call x1, Pallas kernels, per_device(): pl.pallas_call(functools.partial(embed_kernel, **where), out_shape=[pltpu...  1.67 us
    ppermute x1, starting transfers between devices, per_device(): other = lax.ppermute(part, 'fsdp', [(i, i ^ 1) for i in range(copies)])  1.53 us
    ppermute x2, waiting for transfers between devices, swap(): lax.ppermute(rows_to_give, 'patch', [pair for i in range(low, patches - 1...  1.18 us
    ppermute x1, waiting for transfers between devices, per_device(): got = lax.ppermute(send, 'sub', [(0, 1), (1, 0)])  0.9 us
  transfers between devices with their start and end apart: 4, of which 3 were waited for; matrix products, arithmetic and copies ran while one was open for 0% of the time, Pallas kernels for 12%

profile of v5, /device:TPU:0, one launch (start us, length us, event | category | flops | bytes accessed | tf_op | source)
XLA Modules:
  0.0 22.6 jit_solution(3391513238818319460)
XLA Ops:
  0.0 0.0 copy-start.1
  0.7 1.7 %embed.1 = (bf16[16,2,64,128]{3,2,1,0:T(8,128)(2,1)S(1)}, bf16[16,2,8,128]{3,2,1,0:T(8,128)(2,1)S(1)}, bf16[16,2,8,128]{3,2,1,0:T(8,128)(2,1)S(1)}) custom-call(f32[1,1]{1,0:T(1,128)} %bitcast.5.now_ref, bf16[16,256,128]{2,1,0:T(8,128)(2,1)} %cond_ref.1, f32[16,256]{1,0:T(8,128)} %noisy_ref.3, f32[1,128]{1,0:T(1,128)} %bitcast.11), custom_call_target="tpu_custom_call" | custom-call | tf_op jit(solution)/shard_map/embed/pallas_call | solution.py:352
  2.4 0.6 %collective-permute-start = (bf16[16,2,8,128]{3,2,1,0:T(8,128)(2,1)S(1)}, bf16[16,2,8,128]{3,2,1,0:T(8,128)(2,1)S(1)}, u32[]{:S(2)}, u32[]{:S(2)}) collective-permute-start(bf16[16,2,8,128]{3,2,1,0:T(8,128)(2,1)S(1)} %get-tuple-element.18), channel_id=1, source_target_pairs={{0,1},{1,0},{2,3},{3,2},{4,5},{5,4},{6,7},{7,6},{8,9},{9,8},{10,11... | collective-permute-start | bytes 196616 | tf_op jit(solution)/shard_map/ppermute | solution.py:376
  3.0 0.9 %collective-permute-done.got_ref = bf16[16,2,8,128]{3,2,1,0:T(8,128)(2,1)S(1)} collective-permute-done((bf16[16,2,8,128]{3,2,1,0:T(8,128)(2,1)S(1)}, bf16[16,2,8,128]{3,2,1,0:T(8,128)(2,1)S(1)}, u32[]{:S(2)}, u32[]{:S(2)}) %collective-permute-start) | collective-permute-done | bytes 65568 | tf_op jit(solution)/shard_map/ppermute | solution.py:376
  3.9 0.1 border.1
  3.9 0.0 copy-start
  3.9 0.0 copy-start.2
  3.9 0.0 copy-start.3
  4.0 0.8 %collective-permute-start.1 = (bf16[5,2,72,128]{3,2,1,0:T(8,128)(2,1)S(1)}, bf16[5,2,72,128]{3,2,1,0:T(8,128)(2,1)S(1)}, u32[]{:S(2)}, u32[]{:S(2)}) collective-permute-start(bf16[5,2,72,128]{3,2,1,0:T(8,128)(2,1)S(1)} %get-tuple-element.19), channel_id=1, source_target_pairs={{4,8},{8,4},{5,9},{9,5},{6,10},{10,6},{7,11},{11,7},{20,24},{24,20... | collective-permute-start | bytes 552968 | tf_op jit(solution)/shard_map/ppermute | solution.py:402
  4.8 5.8 %collective-permute-start.2 = (bf16[5,2,72,128]{3,2,1,0:T(8,128)(2,1)S(1)}, bf16[5,2,72,128]{3,2,1,0:T(8,128)(2,1)S(1)}, u32[]{:S(2)}, u32[]{:S(2)}) collective-permute-start(bf16[5,2,72,128]{3,2,1,0:T(8,128)(2,1)S(1)} %get-tuple-element.20), channel_id=1, source_target_pairs={{0,4},{4,0},{8,12},{12,8},{1,5},{5,1},{9,13},{13,9},{2,6},{6,2},{1... | collective-permute-start | bytes 552968 | tf_op jit(solution)/shard_map/ppermute | solution.py:402
  10.6 0.0 copy-done.1
  10.6 0.2 %pack.1.w_ref = bf16[2,1536,256]{2,1,0:T(8,128)(2,1)S(1)} custom-call(bf16[2,9,128,128]{3,2,1,0:T(8,128)(2,1)S(1)} %copy-done.1), custom_call_target="tpu_custom_call" | custom-call | bytes 2097152 | tf_op jit(solution)/shard_map/pack/pallas_call | solution.py:378
  11.5 0.0 copy-done
  11.5 0.0 copy-done.2
  11.5 0.0 copy-done.3
  11.5 0.0 copy-start.4
  11.5 0.0 copy-start.5
  11.5 0.0 copy-start.6
  11.5 2.5 %inner.1 = (bf16[16,4,72,128]{3,2,1,0:T(8,128)(2,1)S(1)}, bf16[12,2,72,128]{3,2,1,0:T(8,128)(2,1)S(1)}, bf16[6,3,72,256]{3,2,1,0:T(8,128)(2,1)S(1)}, bf16[8,4,72...) custom-call(bf16[16,2,64,128]{3,2,1,0:T(8,128)(2,1)S(1)} %get-tuple-element.16.mine_ref, ...), custom_call_target="tpu_custom_call" | custom-call | flops 1698693120 | bytes 4194304 | tf_op jit(solution)/shard_map/inner/pallas_call | solution.py:409
  14.0 0.0 collective-permute-done.1.odd_ref
  14.1 1.2 %collective-permute-done.2.even_ref = bf16[5,2,72,128]{3,2,1,0:T(8,128)(2,1)S(1)} collective-permute-done((bf16[5,2,72,128]{3,2,1,0:T(8,128)(2,1)S(1)}, bf16[5,2,72,128]{3,2,1,0:T(8,128)(2,1)S(1)}, u32[]{:S(2)}, u32[]{:S(2)}) %collective-permute-start.2) | collective-permute-done | bytes 184352 | tf_op jit(solution)/shard_map/ppermute | solution.py:402
  15.2 0.0 copy-done.4
  15.2 0.0 copy-done.5
  15.2 0.0 copy-done.6
  15.2 3.0 %outer.1 = f32[16,128]{1,0:T(8,128)S(1)} custom-call(f32[1,1]{1,0:T(1,128)} %bitcast.6.now_ref, f32[1,1]{1,0:T(1,128)} %bitcast.7.next_ref, bf16[5,2,72,128]{3,2,1,0:T(8,128)(2,1)S(1)} %collective-permute-done.1.odd_ref, bf16[5,2,72,128]{3,2,1,0:T(8,128)(2,1)S(1)} %collective-permute-done.2.even_ref, bf16[16,4,72,128]{3,2,1,0:T(8,128)(2,1)S(1)} %get-tuple-element.22.xin_ref, ...), custom_call_target="tpu_custom_call" | custom-call | tf_op jit(solution)/shard_map/outer/pallas_call | solution.py:429
  18.3 1.5 %collective-permute-start.3 = (f32[16,128]{1,0:T(8,128)S(1)}, f32[16,128]{1,0:T(8,128)S(1)}, u32[]{:S(2)}, u32[]{:S(2)}) collective-permute-start(f32[16,128]{1,0:T(8,128)S(1)} %outer.1), channel_id=1, source_target_pairs={{0,2},{2,0},{1,3},{3,1},{4,6},{6,4},{5,7},{7,5},{8,10},{10,8},{9,1... | collective-permute-start | bytes 24584 | tf_op jit(solution)/shard_map/ppermute | solution.py:449
  19.8 2.2 %collective-permute-done.3 = f32[16,128]{1,0:T(8,128)S(1)} collective-permute-done((f32[16,128]{1,0:T(8,128)S(1)}, f32[16,128]{1,0:T(8,128)S(1)}, u32[]{:S(2)}, u32[]{:S(2)}) %collective-permute-start.3) | collective-permute-done | bytes 8224 | tf_op jit(solution)/shard_map/ppermute | solution.py:449
  22.0 0.6 %maximum_select_fusion = f32[16,256]{1,0:T(8,128)} fusion(f32[16,128]{1,0:T(8,128)S(1)} %collective-permute-done.3, f32[16,128]{1,0:T(8,128)S(1)} %outer.1, pred[]{:T(512)S(6)} %eq.3), kind=kLoop, calls=%fused_computation | loop fusion | flops 12288 | bytes 32769 | tf_op jit(solution)/shard_map/jit(_where)/select_n | solution.py:451
Async XLA Ops:
  0.0 10.6 %copy-start.1 = (bf16[2,9,128,128]{3,2,1,0:T(8,128)(2,1)S(1)}, bf16[2,9,128,128]{3,2,1,0:T(8,128)(2,1)}, u32[]{:S(2)}) copy-start(bf16[2,9,128,128]{3,2,1,0:T(8,128)(2,1)} %fine_ref.1) | copy-start | bytes 1769476
  2.4 1.5 %collective-permute-start = (bf16[16,2,8,128]{3,2,1,0:T(8,128)(2,1)S(1)}, bf16[16,2,8,128]{3,2,1,0:T(8,128)(2,1)S(1)}, u32[]{:S(2)}, u32[]{:S(2)}) collective-permute-start(bf16[16,2,8,128]{3,2,1,0:T(8,128)(2,1)S(1)} %get-tuple-element.18), channel_id=1, source_target_pairs={{0,1},{1,0},{2,3},{3,2},{4,5},{5,4},{6,7},{7,6},{8,9},{9,8},{10,11... | collective-permute-start | bytes 196616 | tf_op jit(solution)/shard_map/ppermute | solution.py:376
  3.9 7.5 %copy-start = (bf16[9,256,256]{2,1,0:T(8,128)(2,1)S(1)}, bf16[9,256,256]{2,1,0:T(8,128)(2,1)}, u32[]{:S(2)}) copy-start(bf16[9,256,256]{2,1,0:T(8,128)(2,1)} %param.18) | copy-start | bytes 3538948
  3.9 7.5 %copy-start.2 = (bf16[128,256]{1,0:T(8,128)(2,1)S(1)}, bf16[128,256]{1,0:T(8,128)(2,1)}, u32[]{:S(2)}) copy-start(bf16[128,256]{1,0:T(8,128)(2,1)} %down_ref.3) | copy-start | bytes 196612
  3.9 7.5 %copy-start.3 = (bf16[256,128]{1,0:T(8,128)(2,1)S(1)}, bf16[256,128]{1,0:T(8,128)(2,1)}, u32[]{:S(2)}) copy-start(bf16[256,128]{1,0:T(8,128)(2,1)} %up_ref.3) | copy-start | bytes 196612
  4.0 10.1 %collective-permute-start.1 = (bf16[5,2,72,128]{3,2,1,0:T(8,128)(2,1)S(1)}, bf16[5,2,72,128]{3,2,1,0:T(8,128)(2,1)S(1)}, u32[]{:S(2)}, u32[]{:S(2)}) collective-permute-start(bf16[5,2,72,128]{3,2,1,0:T(8,128)(2,1)S(1)} %get-tuple-element.19), channel_id=1, source_target_pairs={{4,8},{8,4},{5,9},{9,5},{6,10},{10,6},{7,11},{11,7},{20,24},{24,20... | collective-permute-start | bytes 552968 | tf_op jit(solution)/shard_map/ppermute | solution.py:402
  4.8 10.5 %collective-permute-start.2 = (bf16[5,2,72,128]{3,2,1,0:T(8,128)(2,1)S(1)}, bf16[5,2,72,128]{3,2,1,0:T(8,128)(2,1)S(1)}, u32[]{:S(2)}, u32[]{:S(2)}) collective-permute-start(bf16[5,2,72,128]{3,2,1,0:T(8,128)(2,1)S(1)} %get-tuple-element.20), channel_id=1, source_target_pairs={{0,4},{4,0},{8,12},{12,8},{1,5},{5,1},{9,13},{13,9},{2,6},{6,2},{1... | collective-permute-start | bytes 552968 | tf_op jit(solution)/shard_map/ppermute | solution.py:402
  11.5 3.8 %copy-start.4 = (f32[16,256]{1,0:T(8,128)S(1)}, f32[16,256]{1,0:T(8,128)}, u32[]{:S(2)}) copy-start(f32[16,256]{1,0:T(8,128)} %noisy_ref.3) | copy-start | bytes 49156
  11.5 3.7 %copy-start.5 = (f32[16,256]{1,0:T(8,128)S(1)}, f32[16,256]{1,0:T(8,128)}, u32[]{:S(2)}) copy-start(f32[16,256]{1,0:T(8,128)} %noise_ref.1) | copy-start | bytes 49156
  11.5 3.7 %copy-start.6 = (bf16[128]{0:T(256)(128)(2,1)S(1)}, bf16[128]{0:T(256)(128)(2,1)}, u32[]{:S(2)}) copy-start(bf16[128]{0:T(256)(128)(2,1)} %param.21) | copy-start | bytes 772
  18.3 3.7 %collective-permute-start.3 = (f32[16,128]{1,0:T(8,128)S(1)}, f32[16,128]{1,0:T(8,128)S(1)}, u32[]{:S(2)}, u32[]{:S(2)}) collective-permute-start(f32[16,128]{1,0:T(8,128)S(1)} %outer.1), channel_id=1, source_target_pairs={{0,2},{2,0},{1,3},{3,1},{4,6},{6,4},{5,7},{7,5},{8,10},{10,8},{9,1... | collective-permute-start | bytes 24584 | tf_op jit(solution)/shard_map/ppermute | solution.py:449

commit v6 on v5

--- a/solution.py
+++ b/solution.py
@@ -68,23 +68,39 @@
         copy.wait()
     level = now_ref[...]
     scale_in = 1.0 / jnp.sqrt(level * level + 1.0)
-    turned[:, :rows] = jnp.transpose(field[...] * scale_in)
+    scaled = field[...] * scale_in
+    high = scaled.astype(BF16).astype(F32)
+    middle = (scaled - high).astype(BF16).astype(F32)
+    low = scaled - high - middle
+    fill = jnp.zeros((128 - 3 * rows, cols), F32)
+    turned[...] = jnp.transpose(jnp.concatenate([high, middle, low, fill], axis=0)).astype(BF16)
     proj = embedding[...]
+    c1 = proj.shape[1]
     head = lax.broadcasted_iota(jnp.int32, (PER, 128), 0) < PER // 2
 
-    def hidden(buf, r, at):
-        return buf[r].astype(F32) + turned[pl.ds(at, buf.shape[1]), r : r + 1] * proj
-
+    lhs = jnp.concatenate([turned[pl.ds(at, n)] for at, n in ((start, window), (given, EDGE), (near_by, EDGE))], axis=0)
+    term = lax.broadcasted_iota(jnp.int32, (128, 2 * c1), 0)
+    right_half = jnp.where(lax.broadcasted_iota(jnp.int32, (128, 2 * c1), 1) < c1, 0, 1)
+    for r in range(0, rows, 2):
+        wanted = right_half + r
+        pick = jnp.where(term == wanted, 1.0, 0.0)
+        for k in (1, 2):
+            pick = jnp.where(term == wanted + k * rows, 1.0, pick)
+        spread = jnp.dot(lhs, pick.astype(BF16), preferred_element_type=F32)
+        for o in range(2):
+            product = spread[:, o * c1 : (o + 1) * c1] * proj
+            wide[r + o] = product[:window]
+            edge[r + o] = product[window:]
     for copy in copies[:-1]:
         copy.wait()
     for r in range(rows):
-        edge[r % 2, :EDGE] = hidden(give, r, given)
+        edge[r, :EDGE] = give[r].astype(F32) + edge[r, :EDGE]
         for q in range(2):
-            send_ref[r, q] = edge[r % 2, pl.ds(q, PER, stride=2), :].astype(BF16)
+            send_ref[r, q] = edge[r, pl.ds(q, PER, stride=2), :].astype(BF16)
         if pieces > 1:
-            edge[r % 2, EDGE:] = hidden(inner, r, near_by)
+            edge[r, EDGE:] = inner[r].astype(F32) + edge[r, EDGE:]
             for q in range(2):
-                block = edge[r % 2, pl.ds(EDGE + q, PER, stride=2), :]
+                block = edge[r, pl.ds(EDGE + q, PER, stride=2), :]
                 to_right = block * flag(jnp.logical_not(place.last))
                 to_left = block * flag(jnp.logical_not(place.first))
                 tile_ref[r, q] = jnp.where(head, to_right, to_left).astype(BF16)
@@ -92,9 +108,9 @@
             tile_ref[r] = jnp.zeros_like(tile_ref[r])
     copies[-1].wait()
     for r in range(rows):
-        wide[r % 2] = hidden(main, r, start)
+        wide[r] = main[r].astype(F32) + wide[r]
         for q in range(2):
-            mine_ref[r, q] = wide[r % 2, pl.ds(q, window // 2, stride=2), :].astype(BF16)
+            mine_ref[r, q] = wide[r, pl.ds(q, window // 2, stride=2), :].astype(BF16)
 
 
 def border_kernel(mine_ref, tile_ref, got_ref, full_ref, even_ref, odd_ref, *, sizes, pieces):
@@ -339,7 +355,7 @@
     c2 = down_proj.shape[1]
     patches, copies = sizes["patch"], sizes["fsdp"]
     pieces = 2 if copies % 2 == 0 and cols % 256 == 0 else 1
-    if sizes["sub"] != 2 or rows < 16:
+    if sizes["sub"] != 2 or rows < 16 or rows > 42 or rows % 2:
         raise ValueError("unsupported split")
     window = cols // pieces
     own = window // 2
@@ -364,9 +380,9 @@
             pltpu.VMEM((rows, EDGE, c1), BF16),
             pltpu.VMEM((rows, cols), F32),
             pltpu.VMEM((1, c1), F32),
-            pltpu.VMEM((cols, 128), F32),
-            pltpu.VMEM((2, window, c1), F32),
-            pltpu.VMEM((2, 2 * EDGE, c1), F32),
+            pltpu.VMEM((cols, 128), BF16),
+            pltpu.VMEM((rows, window, c1), F32),
+            pltpu.VMEM((rows, 2 * EDGE, c1), F32),
             pltpu.SemaphoreType.DMA((5,)),
         ],
         compiler_params=limit(8),

time: 22.8 us -> 22.7 us (level)
  no operation moved by 1% of the time
where the time goes in v6:
time: 22.7 us; the launch traced here: 22.4 us
  starting transfers between devices  8.68 us (38%)
  Pallas kernels  7.35 us (32%)
  waiting for transfers between devices  4.24 us (19%)
  between operations  1.48 us (7%)
  other arithmetic  0.61 us (3%)
    ppermute x2, starting transfers between devices, swap(): lax.ppermute(rows_to_give, 'patch', [pair for i in range(low, patches - 1...  6.6 us
    pallas_call x1, Pallas kernels, per_device(): pl.pallas_call(functools.partial(outer_kernel, **where), out_shape=pltpu....  3.05 us
    pallas_call x1, Pallas kernels, per_device(): pl.pallas_call(functools.partial(inner_kernel, **where), out_shape=[pltpu...  2.52 us
    ppermute x1, waiting for transfers between devices, per_device(): other = lax.ppermute(part, 'fsdp', [(i, i ^ 1) for i in range(copies)])  2.16 us
    ppermute x1, starting transfers between devices, per_device(): other = lax.ppermute(part, 'fsdp', [(i, i ^ 1) for i in range(copies)])  1.53 us
    pallas_call x1, Pallas kernels, per_device(): pl.pallas_call(functools.partial(embed_kernel, **where), out_shape=[pltpu...  1.49 us
    ppermute x2, waiting for transfers between devices, swap(): lax.ppermute(rows_to_give, 'patch', [pair for i in range(low, patches - 1...  1.18 us
    ppermute x1, waiting for transfers between devices, per_device(): got = lax.ppermute(send, 'sub', [(0, 1), (1, 0)])  0.9 us
  transfers between devices with their start and end apart: 4, of which 3 were waited for; matrix products, arithmetic and copies ran while one was open for 0% of the time, Pallas kernels for 12%

profile of v6, /device:TPU:0, one launch (start us, length us, event | category | flops | bytes accessed | tf_op | source)
XLA Modules:
  0.0 22.4 jit_solution(1794750194309036604)
XLA Ops:
  0.0 0.0 copy-start.1
  0.7 1.5 %embed.1 = (bf16[16,2,64,128]{3,2,1,0:T(8,128)(2,1)S(1)}, bf16[16,2,8,128]{3,2,1,0:T(8,128)(2,1)S(1)}, bf16[16,2,8,128]{3,2,1,0:T(8,128)(2,1)S(1)}) custom-call(f32[1,1]{1,0:T(1,128)} %bitcast.5.now_ref, bf16[16,256,128]{2,1,0:T(8,128)(2,1)} %cond_ref.1, f32[16,256]{1,0:T(8,128)} %noisy_ref.3, f32[1,128]{1,0:T(1,128)} %bitcast.11), custom_call_target="tpu_custom_call" | custom-call | tf_op jit(solution)/shard_map/embed/pallas_call | solution.py:368
  2.2 0.6 %collective-permute-start = (bf16[16,2,8,128]{3,2,1,0:T(8,128)(2,1)S(1)}, bf16[16,2,8,128]{3,2,1,0:T(8,128)(2,1)S(1)}, u32[]{:S(2)}, u32[]{:S(2)}) collective-permute-start(bf16[16,2,8,128]{3,2,1,0:T(8,128)(2,1)S(1)} %get-tuple-element.18), channel_id=1, source_target_pairs={{0,1},{1,0},{2,3},{3,2},{4,5},{5,4},{6,7},{7,6},{8,9},{9,8},{10,11... | collective-permute-start | bytes 196616 | tf_op jit(solution)/shard_map/ppermute | solution.py:392
  2.8 0.9 %collective-permute-done.got_ref = bf16[16,2,8,128]{3,2,1,0:T(8,128)(2,1)S(1)} collective-permute-done((bf16[16,2,8,128]{3,2,1,0:T(8,128)(2,1)S(1)}, bf16[16,2,8,128]{3,2,1,0:T(8,128)(2,1)S(1)}, u32[]{:S(2)}, u32[]{:S(2)}) %collective-permute-start) | collective-permute-done | bytes 65568 | tf_op jit(solution)/shard_map/ppermute | solution.py:392
  3.7 0.1 border.1
  3.7 0.0 copy-start
  3.7 0.0 copy-start.2
  3.8 0.0 copy-start.3
  3.8 0.8 %collective-permute-start.1 = (bf16[5,2,72,128]{3,2,1,0:T(8,128)(2,1)S(1)}, bf16[5,2,72,128]{3,2,1,0:T(8,128)(2,1)S(1)}, u32[]{:S(2)}, u32[]{:S(2)}) collective-permute-start(bf16[5,2,72,128]{3,2,1,0:T(8,128)(2,1)S(1)} %get-tuple-element.19), channel_id=1, source_target_pairs={{4,8},{8,4},{5,9},{9,5},{6,10},{10,6},{7,11},{11,7},{20,24},{24,20... | collective-permute-start | bytes 552968 | tf_op jit(solution)/shard_map/ppermute | solution.py:418
  4.6 5.8 %collective-permute-start.2 = (bf16[5,2,72,128]{3,2,1,0:T(8,128)(2,1)S(1)}, bf16[5,2,72,128]{3,2,1,0:T(8,128)(2,1)S(1)}, u32[]{:S(2)}, u32[]{:S(2)}) collective-permute-start(bf16[5,2,72,128]{3,2,1,0:T(8,128)(2,1)S(1)} %get-tuple-element.20), channel_id=1, source_target_pairs={{0,4},{4,0},{8,12},{12,8},{1,5},{5,1},{9,13},{13,9},{2,6},{6,2},{1... | collective-permute-start | bytes 552968 | tf_op jit(solution)/shard_map/ppermute | solution.py:418
  10.4 0.0 copy-done.1
  10.4 0.2 %pack.1.w_ref = bf16[2,1536,256]{2,1,0:T(8,128)(2,1)S(1)} custom-call(bf16[2,9,128,128]{3,2,1,0:T(8,128)(2,1)S(1)} %copy-done.1), custom_call_target="tpu_custom_call" | custom-call | bytes 2097152 | tf_op jit(solution)/shard_map/pack/pallas_call | solution.py:394
  11.3 0.0 copy-done
  11.3 0.0 copy-done.2
  11.3 0.0 copy-done.3
  11.3 0.0 copy-start.4
  11.3 0.0 copy-start.5
  11.3 0.0 copy-start.6
  11.3 2.5 %inner.1 = (bf16[16,4,72,128]{3,2,1,0:T(8,128)(2,1)S(1)}, bf16[12,2,72,128]{3,2,1,0:T(8,128)(2,1)S(1)}, bf16[6,3,72,256]{3,2,1,0:T(8,128)(2,1)S(1)}, bf16[8,4,72...) custom-call(bf16[16,2,64,128]{3,2,1,0:T(8,128)(2,1)S(1)} %get-tuple-element.16.mine_ref, ...), custom_call_target="tpu_custom_call" | custom-call | flops 1698693120 | bytes 4194304 | tf_op jit(solution)/shard_map/inner/pallas_call | solution.py:425
  13.9 0.0 collective-permute-done.1.odd_ref
  13.9 1.2 %collective-permute-done.2.even_ref = bf16[5,2,72,128]{3,2,1,0:T(8,128)(2,1)S(1)} collective-permute-done((bf16[5,2,72,128]{3,2,1,0:T(8,128)(2,1)S(1)}, bf16[5,2,72,128]{3,2,1,0:T(8,128)(2,1)S(1)}, u32[]{:S(2)}, u32[]{:S(2)}) %collective-permute-start.2) | collective-permute-done | bytes 184352 | tf_op jit(solution)/shard_map/ppermute | solution.py:418
  15.0 0.0 copy-done.4
  15.1 0.0 copy-done.5
  15.1 0.0 copy-done.6
  15.1 3.1 %outer.1 = f32[16,128]{1,0:T(8,128)S(1)} custom-call(f32[1,1]{1,0:T(1,128)} %bitcast.6.now_ref, f32[1,1]{1,0:T(1,128)} %bitcast.7.next_ref, bf16[5,2,72,128]{3,2,1,0:T(8,128)(2,1)S(1)} %collective-permute-done.1.odd_ref, bf16[5,2,72,128]{3,2,1,0:T(8,128)(2,1)S(1)} %collective-permute-done.2.even_ref, bf16[16,4,72,128]{3,2,1,0:T(8,128)(2,1)S(1)} %get-tuple-element.22.xin_ref, ...), custom_call_target="tpu_custom_call" | custom-call | tf_op jit(solution)/shard_map/outer/pallas_call | solution.py:445
  18.1 1.5 %collective-permute-start.3 = (f32[16,128]{1,0:T(8,128)S(1)}, f32[16,128]{1,0:T(8,128)S(1)}, u32[]{:S(2)}, u32[]{:S(2)}) collective-permute-start(f32[16,128]{1,0:T(8,128)S(1)} %outer.1), channel_id=1, source_target_pairs={{0,2},{2,0},{1,3},{3,1},{4,6},{6,4},{5,7},{7,5},{8,10},{10,8},{9,1... | collective-permute-start | bytes 24584 | tf_op jit(solution)/shard_map/ppermute | solution.py:465
  19.6 2.2 %collective-permute-done.3 = f32[16,128]{1,0:T(8,128)S(1)} collective-permute-done((f32[16,128]{1,0:T(8,128)S(1)}, f32[16,128]{1,0:T(8,128)S(1)}, u32[]{:S(2)}, u32[]{:S(2)}) %collective-permute-start.3) | collective-permute-done | bytes 8224 | tf_op jit(solution)/shard_map/ppermute | solution.py:465
  21.8 0.6 %maximum_select_fusion = f32[16,256]{1,0:T(8,128)} fusion(f32[16,128]{1,0:T(8,128)S(1)} %collective-permute-done.3, f32[16,128]{1,0:T(8,128)S(1)} %outer.1, pred[]{:T(512)S(6)} %eq.3), kind=kLoop, calls=%fused_computation | loop fusion | flops 12288 | bytes 32769 | tf_op jit(solution)/shard_map/jit(_where)/select_n | solution.py:467
Async XLA Ops:
  0.0 10.4 %copy-start.1 = (bf16[2,9,128,128]{3,2,1,0:T(8,128)(2,1)S(1)}, bf16[2,9,128,128]{3,2,1,0:T(8,128)(2,1)}, u32[]{:S(2)}) copy-start(bf16[2,9,128,128]{3,2,1,0:T(8,128)(2,1)} %fine_ref.1) | copy-start | bytes 1769476
  2.2 1.5 %collective-permute-start = (bf16[16,2,8,128]{3,2,1,0:T(8,128)(2,1)S(1)}, bf16[16,2,8,128]{3,2,1,0:T(8,128)(2,1)S(1)}, u32[]{:S(2)}, u32[]{:S(2)}) collective-permute-start(bf16[16,2,8,128]{3,2,1,0:T(8,128)(2,1)S(1)} %get-tuple-element.18), channel_id=1, source_target_pairs={{0,1},{1,0},{2,3},{3,2},{4,5},{5,4},{6,7},{7,6},{8,9},{9,8},{10,11... | collective-permute-start | bytes 196616 | tf_op jit(solution)/shard_map/ppermute | solution.py:392
  3.7 7.5 %copy-start = (bf16[9,256,256]{2,1,0:T(8,128)(2,1)S(1)}, bf16[9,256,256]{2,1,0:T(8,128)(2,1)}, u32[]{:S(2)}) copy-start(bf16[9,256,256]{2,1,0:T(8,128)(2,1)} %param.18) | copy-start | bytes 3538948
  3.7 7.5 %copy-start.2 = (bf16[128,256]{1,0:T(8,128)(2,1)S(1)}, bf16[128,256]{1,0:T(8,128)(2,1)}, u32[]{:S(2)}) copy-start(bf16[128,256]{1,0:T(8,128)(2,1)} %down_ref.3) | copy-start | bytes 196612
  3.8 7.5 %copy-start.3 = (bf16[256,128]{1,0:T(8,128)(2,1)S(1)}, bf16[256,128]{1,0:T(8,128)(2,1)}, u32[]{:S(2)}) copy-start(bf16[256,128]{1,0:T(8,128)(2,1)} %up_ref.3) | copy-start | bytes 196612
  3.8 10.1 %collective-permute-start.1 = (bf16[5,2,72,128]{3,2,1,0:T(8,128)(2,1)S(1)}, bf16[5,2,72,128]{3,2,1,0:T(8,128)(2,1)S(1)}, u32[]{:S(2)}, u32[]{:S(2)}) collective-permute-start(bf16[5,2,72,128]{3,2,1,0:T(8,128)(2,1)S(1)} %get-tuple-element.19), channel_id=1, source_target_pairs={{4,8},{8,4},{5,9},{9,5},{6,10},{10,6},{7,11},{11,7},{20,24},{24,20... | collective-permute-start | bytes 552968 | tf_op jit(solution)/shard_map/ppermute | solution.py:418
  4.6 10.5 %collective-permute-start.2 = (bf16[5,2,72,128]{3,2,1,0:T(8,128)(2,1)S(1)}, bf16[5,2,72,128]{3,2,1,0:T(8,128)(2,1)S(1)}, u32[]{:S(2)}, u32[]{:S(2)}) collective-permute-start(bf16[5,2,72,128]{3,2,1,0:T(8,128)(2,1)S(1)} %get-tuple-element.20), channel_id=1, source_target_pairs={{0,4},{4,0},{8,12},{12,8},{1,5},{5,1},{9,13},{13,9},{2,6},{6,2},{1... | collective-permute-start | bytes 552968 | tf_op jit(solution)/shard_map/ppermute | solution.py:418
  11.3 3.8 %copy-start.4 = (f32[16,256]{1,0:T(8,128)S(1)}, f32[16,256]{1,0:T(8,128)}, u32[]{:S(2)}) copy-start(f32[16,256]{1,0:T(8,128)} %noisy_ref.3) | copy-start | bytes 49156
  11.3 3.7 %copy-start.5 = (f32[16,256]{1,0:T(8,128)S(1)}, f32[16,256]{1,0:T(8,128)}, u32[]{:S(2)}) copy-start(f32[16,256]{1,0:T(8,128)} %noise_ref.1) | copy-start | bytes 49156
  11.3 3.7 %copy-start.6 = (bf16[128]{0:T(256)(128)(2,1)S(1)}, bf16[128]{0:T(256)(128)(2,1)}, u32[]{:S(2)}) copy-start(bf16[128]{0:T(256)(128)(2,1)} %param.21) | copy-start | bytes 772
  18.1 3.7 %collective-permute-start.3 = (f32[16,128]{1,0:T(8,128)S(1)}, f32[16,128]{1,0:T(8,128)S(1)}, u32[]{:S(2)}, u32[]{:S(2)}) collective-permute-start(f32[16,128]{1,0:T(8,128)S(1)} %outer.1), channel_id=1, source_target_pairs={{0,2},{2,0},{1,3},{3,1},{4,6},{6,4},{5,7},{7,5},{8,10},{10,8},{9,1... | collective-permute-start | bytes 24584 | tf_op jit(solution)/shard_map/ppermute | solution.py:465
